TPU v7x, 32 devices: a whole 2x2x4 slice. The times are simulated.
32 devices in a mesh: days: 2 (over x), sta: 16 (over z, y, core).
Axes of the slice: x: 2, y: 2, z: 4, core: 2. Of those that a mesh axis runs over, the one named last changes fastest.
Arguments:
- records: bfloat16 [384, 256, 256], P(('days', 'sta')), parts along dimension 0, may hold values from -330 to 330
- counts: int32 [128, 4], P(('days', 'sta')), parts along dimension 0, may hold values from 0 to 64
- gap_mask: int32 [128, 256], P(('days', 'sta')), parts along dimension 0, may hold values 0 or 1
Outputs:
- cross_spectra: bfloat16 [7, 2, 384, 12, 128], P(None, None, ('days', 'sta')), parts along dimension 2
There are 2 independent parts, one for each index of `days`. A program takes and returns all parts, laid end to end along the dimension named above; each array names one. Nothing has to cross between parts.
All inputs are finite; a program needn't handle non-finite values. No bound on the sum of `gap_mask` on one device may be relied on, other than what follows from the above.
Results may differ from a plain program's by a relative error of at most 0.0062.
Values may be sent and summed in bfloat16 or wider, within the bound.
No kernel may reach another device: no remote copies, remote signals or barrier semaphores. Data moves between devices by JAX's collectives and lax.ppermute only.
A program may use at most 64 MiB of HBM per device.

v0:
```python
import math

import jax
import jax.numpy as jnp
import numpy as np
from jax import lax
from jax.experimental import pallas as pl
from jax.experimental.pallas import tpu as pltpu
from jax.sharding import PartitionSpec as P


ROUNDS = 3
LANES = 128
PITCH = 16
SKEW = 8
MIB = 1 << 20
PAIR_LIMIT = 10 * MIB
PAIR_COST = pl.CostEstimate(flops=3_000_000_000, transcendentals=0, bytes_accessed=12_000_000)
WHITEN_COST = pl.CostEstimate(flops=2_000_000_000, transcendentals=0, bytes_accessed=8_000_000)

epsilon = 1e-06

NT = (((1,), (1,)), ((), ()))


def fourier_matrix(samples):
    freq_bins = samples // 2
    times_axis = np.arange(samples, dtype=np.int32)
    bins_axis = np.arange(freq_bins, dtype=np.int32)
    phase_idx = times_axis[:, None] * bins_axis[None, :] % samples
    step = np.float32(2.0 * math.pi / samples)
    angle = step * phase_idx.astype(np.float32)
    half = np.float32(0.5)
    taper = half - half * np.cos(step * (times_axis.astype(np.float32) + half))
    table_re = taper[:, None] * np.cos(angle)
    table_im = -taper[:, None] * np.sin(angle)
    return jnp.asarray(np.concatenate([table_re.T, table_im.T], axis=0).astype(jnp.bfloat16))


def lane_iota(rows):
    return lax.broadcasted_iota(jnp.int32, (rows, LANES), 1)


def validity_rows(hour, seg_hour, counts_ref, gap_ref):
    stations = gap_ref.shape[0]
    per_tile = LANES // seg_hour
    tile = gap_ref[:, pl.ds(hour // per_tile * LANES, LANES)].astype(jnp.float32)
    turned = pltpu.roll(tile, seg_hour, 1)
    lane = lane_iota(stations)
    low = lane < seg_hour
    doubled = jnp.where(low, tile, turned) if hour % per_tile == 0 else jnp.where(low, turned, tile)
    position = jnp.where(low, lane, lane - seg_hour)
    return [
        jnp.where(
            position[station : station + 1] < counts_ref[station, hour],
            doubled[station : station + 1],
            0.0,
        )
        for station in range(stations)
    ]


def whiten_block(records_ref, valid, table_ref, out_ref):
    channels, seg_hour, samples = records_ref.shape
    bins = samples // 2
    row = lax.broadcasted_iota(jnp.int32, (bins, LANES), 0)
    low_side = lane_iota(bins) < seg_hour
    slot = jnp.logical_and(row == 0, jnp.logical_not(low_side))
    table = table_ref[...]
    per_station = channels // len(valid)
    first_half = lane_iota(1) < seg_hour
    for channel in range(0, channels, 2):
        both = jnp.concatenate([records_ref[channel], records_ref[channel + 1]], axis=0)
        spectrum = lax.dot_general(table, both, NT, preferred_element_type=jnp.float32)
        power = jnp.sum(spectrum * spectrum, axis=0, keepdims=True) * (1.0 / samples)
        pair_valid = jnp.where(
            first_half, valid[channel // per_station], valid[(channel + 1) // per_station]
        )
        scaled = spectrum * (lax.rsqrt(power + epsilon) * pair_valid)
        real, imag = scaled[:bins], scaled[bins:]
        one = jnp.where(low_side, real, pltpu.roll(imag, seg_hour, 1))
        two = jnp.where(low_side, pltpu.roll(real, seg_hour, 1), imag)
        for value, at in ((one, channel), (two, channel + 1)):
            value = jnp.where(slot, valid[at // per_station], value)
            out_ref[at] = value.astype(jnp.bfloat16)


def whiten_first_kernel(counts_hbm, records_hbm, gap_hbm, table_hbm, *refs):
    out_ref, rest_ref, valid_ref, table_ref, counts_ref, records_ref, gap_ref, sems = refs
    seg_hour = records_ref.shape[1]
    hours = valid_ref.shape[0]

    def hour_of(hour):
        return records_hbm.at[:, pl.ds(hour * seg_hour, seg_hour), :]

    moves = [
        (counts_hbm, counts_ref),
        (gap_hbm, gap_ref),
        (table_hbm, table_ref),
        (hour_of(0), records_ref),
    ]
    now = len(moves)
    moves += [(hour_of(hour), rest_ref.at[hour - 1]) for hour in range(1, hours)]
    copies = [
        pltpu.make_async_copy(source, target, sems.at[i])
        for i, (source, target) in enumerate(moves)
    ]
    for copy in copies:
        copy.start()
    for copy in copies[:now]:
        copy.wait()
    valid = [validity_rows(hour, seg_hour, counts_ref, gap_ref) for hour in range(hours)]
    for hour in range(1, hours):
        for station, row in enumerate(valid[hour]):
            valid_ref[hour, station : station + 1, :] = row
    whiten_block(records_ref, valid[0], table_ref, out_ref)
    for copy in copies[now:]:
        copy.wait()


def whiten_first(records, counts, gap_mask, table):
    channels, segments, samples = records.shape
    stations, hours = counts.shape
    seg_hour = segments // hours
    hbm = pl.BlockSpec(memory_space=pltpu.HBM)
    vmem = pl.BlockSpec(memory_space=pltpu.VMEM)
    block = (channels, seg_hour, samples)
    return pl.pallas_call(
        whiten_first_kernel,
        out_shape=[
            jax.ShapeDtypeStruct((channels, samples // 2, LANES), jnp.bfloat16),
            jax.ShapeDtypeStruct((hours - 1, *block), records.dtype),
            jax.ShapeDtypeStruct((hours, stations, LANES), jnp.float32),
            jax.ShapeDtypeStruct(table.shape, table.dtype),
        ],
        in_specs=[hbm] * 4,
        out_specs=[vmem] * 4,
        scratch_shapes=[
            pltpu.SMEM(counts.shape, counts.dtype),
            pltpu.VMEM(block, records.dtype),
            pltpu.VMEM(gap_mask.shape, gap_mask.dtype),
            pltpu.SemaphoreType.DMA((hours + 3,)),
        ],
        cost_estimate=WHITEN_COST,
        compiler_params=pltpu.CompilerParams(vmem_limit_bytes=4 * MIB),
        name="whiten_first",
    )(
        *(
            pltpu.with_memory_space_constraint(x, pltpu.HBM)
            for x in (counts, records, gap_mask, table)
        )
    )


def whiten_hour_kernel(hour, rest_ref, valid_ref, table_ref, out_ref):
    valid = [valid_ref[hour, station : station + 1, :] for station in range(valid_ref.shape[1])]
    whiten_block(rest_ref.at[hour - 1], valid, table_ref, out_ref)


def whiten_hour(rest, valid, table, hour):
    _, channels, _, samples = rest.shape
    vmem = pl.BlockSpec(memory_space=pltpu.VMEM)
    return pl.pallas_call(
        lambda *refs: whiten_hour_kernel(hour, *refs),
        out_shape=jax.ShapeDtypeStruct((channels, samples // 2, LANES), jnp.bfloat16),
        in_specs=[vmem] * 3,
        out_specs=vmem,
        cost_estimate=WHITEN_COST,
        compiler_params=pltpu.CompilerParams(vmem_limit_bytes=4 * MIB),
        name="whiten_hour",
    )(rest, valid, table)


def pair_hour_kernel(hours, first, last, mirrored, *refs):
    refs = list(refs)
    blocks = [refs.pop(0) for _ in range(ROUNDS + 1)]
    before_ref = None if first else refs.pop(0)
    channels, bins, _ = blocks[0].shape
    half = LANES // 2
    if last:
        kept_ref, *back_refs, wide_ref, acc_ref, back_f32 = refs
    else:
        acc_ref, wide_ref = refs
    pitch = bins + SKEW
    for q, block in enumerate(blocks):
        for channel in range(channels):
            start = (q * channels + channel) * pitch
            wide_ref[start : start + bins, :] = block[channel].astype(jnp.float32)
    for pad in range(PITCH - channels):
        start = (len(blocks) * channels + pad) * pitch
        wide_ref[start : start + bins, :] = jnp.zeros((bins, LANES), jnp.float32)

    def tile_at(q, k):
        return wide_ref[pl.ds(q * channels * pitch + k, PITCH, stride=pitch), :]

    low = lane_iota(PITCH) < half
    zeroth = [tile_at(q, 0) for q in range(len(blocks))]
    valid = [jnp.where(low, pltpu.roll(t, half, 1), t).astype(jnp.bfloat16) for t in zeroth]
    for q, t in enumerate(zeroth):
        wide_ref[pl.ds(q * channels * pitch, PITCH, stride=pitch), :] = jnp.where(low, t, 0.0)
    joint = 0.5 * lax.dot_general(
        valid[0], jnp.concatenate(valid + valid, axis=0), NT, preferred_element_type=jnp.float32
    )
    weight = 1.0 / (hours * jnp.maximum(joint, 1.0))
    weight = jnp.concatenate([weight, weight], axis=0)
    sign = jnp.where(low, 1.0, -1.0)
    low_product = lane_iota(2 * PITCH) < half
    half_bins = bins // 2

    def step(k, carry):
        left, right = [], []
        for part in range(2):
            tiles = [tile_at(q, k + part * half_bins) for q in range(len(blocks))]
            turned = pltpu.roll(tiles[0], half, 1) * sign
            tiles = [t.astype(jnp.bfloat16) for t in tiles]
            left += [tiles[0], turned.astype(jnp.bfloat16)]
            right += tiles
        product = lax.dot_general(
            jnp.concatenate(left, axis=0),
            jnp.concatenate(right, axis=0),
            NT,
            preferred_element_type=jnp.float32,
        )
        product = weight * jnp.where(low_product, product[: 2 * PITCH], product[2 * PITCH :])
        place = pl.ds(pl.multiple_of(k * 2 * PITCH, 2 * PITCH), 2 * PITCH)
        if not first:
            product = product + before_ref[place, :]
        acc_ref[place, :] = product
        return carry

    lax.fori_loop(0, half_bins, step, 0, unroll=half_bins)
    if not last:
        return
    low_half = lane_iota(half) < half
    distances = distances_of(mirrored)

    def finish(a, carry):
        both = jnp.concatenate(
            [
                acc_ref[pl.ds(part * PITCH + a, half_bins, stride=2 * PITCH), :]
                for part in range(2)
            ],
            axis=0,
        )
        by_bin = both.T
        upper, lower = by_bin[:half], by_bin[half:]
        real = jnp.where(low_half, upper, pltpu.roll(lower, half, 1))
        imag = jnp.where(low_half, pltpu.roll(upper, half, 1), lower)
        for part, value in enumerate((real, imag)):
            for q in range(len(blocks)):
                rows = value[q * PITCH : q * PITCH + channels]
                place = pl.ds(a * 2 * channels + part, channels, stride=2)
                if q:
                    kept_ref[distances[q - 1], place, :] = rows
                    back_f32[q - 1, pl.ds(2 * a + part, channels, stride=2 * channels), :] = (
                        -rows if part else rows
                    )
                else:
                    kept_ref[0, place, :] = rows
        return carry

    lax.fori_loop(0, channels, finish, 0, unroll=12)
    for q in range(ROUNDS):
        for d in range(ROUNDS):

            @pl.when(distances[q] == d + 1)
            def _():
                back_refs[d][...] = back_f32[q].astype(jnp.bfloat16)


def pair_hour(blocks, before, hours, last, mirrored):
    channels, bins, lanes = blocks[0].shape
    first = before is None
    acc = (bins // 2 * 2 * PITCH, lanes)
    rows = 2 * channels * channels
    wide = pltpu.VMEM(
        ((len(blocks) * channels + PITCH - channels) * (bins + SKEW), lanes), jnp.float32
    )
    vmem = pl.BlockSpec(memory_space=pltpu.VMEM)
    args, specs = [], []
    args += blocks
    specs += [vmem] * len(blocks)
    if not first:
        args.append(before)
        specs.append(vmem)
    if last:
        out_shape = [
            jax.ShapeDtypeStruct((ROUNDS + 1, rows, lanes), jnp.float32),
            *[jax.ShapeDtypeStruct((rows, lanes), jnp.bfloat16)] * ROUNDS,
        ]
        out_specs = [vmem] * (ROUNDS + 1)
        scratch = [
            wide,
            pltpu.VMEM(acc, jnp.float32),
            pltpu.VMEM((ROUNDS, rows, lanes), jnp.float32),
        ]
    else:
        out_shape = jax.ShapeDtypeStruct(acc, jnp.float32)
        out_specs = vmem
        scratch = [wide]
    return pl.pallas_call(
        lambda *refs: pair_hour_kernel(hours, first, last, mirrored, *refs),
        out_shape=out_shape,
        in_specs=specs,
        out_specs=out_specs,
        scratch_shapes=scratch,
        cost_estimate=PAIR_COST,
        compiler_params=pltpu.CompilerParams(vmem_limit_bytes=PAIR_LIMIT),
        name="pair_hour_last" if last else "pair_hour",
    )(*args)


def put(out_ref, slot, value):
    out_ref[slot] = value.reshape(out_ref.shape[1], 2, LANES).astype(jnp.bfloat16)


def join_below_kernel(behind_ref, ahead_ref, *refs):
    from_rear, out_ref = refs[:ROUNDS], refs[-1]
    put(out_ref, ROUNDS, behind_ref[0] + ahead_ref[0])
    for d in range(1, ROUNDS + 1):
        put(out_ref, ROUNDS - d, behind_ref[d] + from_rear[d - 1][...].astype(jnp.float32))


def join_above_kernel(ahead_ref, *refs):
    from_ahead, out_ref = refs[:ROUNDS], refs[-1]
    for d in range(1, ROUNDS + 1):
        put(out_ref, d - 1, ahead_ref[d] + from_ahead[d - 1][...].astype(jnp.float32))


def join(behind, ahead, from_ahead, from_rear):
    _, rows, lanes = behind.shape
    vmem = pl.BlockSpec(memory_space=pltpu.VMEM)
    out = jax.ShapeDtypeStruct((2 * ROUNDS + 1, rows // 2, 2, lanes), jnp.bfloat16)
    half = (ROUNDS + 1, rows // 2, 2, lanes)
    params = pltpu.CompilerParams(vmem_limit_bytes=4 * MIB)
    below = pl.pallas_call(
        join_below_kernel,
        grid=(1,),
        out_shape=out,
        in_specs=[vmem] * (ROUNDS + 2),
        out_specs=pl.BlockSpec(half, lambda i: (0, 0, 0, 0)),
        compiler_params=params,
        name="join_below",
    )(behind, ahead, *from_rear)
    return pl.pallas_call(
        join_above_kernel,
        grid=(1,),
        out_shape=out,
        in_specs=[vmem] * (ROUNDS + 1) + [pl.BlockSpec(memory_space=pl.ANY)],
        out_specs=pl.BlockSpec(half, lambda i: (1, 0, 0, 0)),
        input_output_aliases={ROUNDS + 1: 0},
        compiler_params=params,
        name="join_above",
    )(ahead, *from_ahead, below)


LEVEL = 4
DISTANCES = ((3, 1, 2), (1, 3, 2), (3, 2, 1), (1, 2, 3))


def send(value, count, mirrored, *hops):
    levels = count // LEVEL
    pairs = [
        (LEVEL * level + source, LEVEL * ((level + up) % levels) + target)
        for source, target, up in hops
        for level in range(levels)
    ]
    if mirrored:
        pairs = [(count - 1 - source, count - 1 - target) for source, target in pairs]
    return lax.ppermute(value, "sta", pairs)


def shift(value, count, steps):
    pairs = [(source, (source + steps) % count) for source in range(count)]
    return lax.ppermute(value, "sta", pairs)


def pick_kernel(role, far_ref, relayed_ref, out_ref):
    mine = lax.rem(lax.axis_index("sta"), LEVEL) == role

    @pl.when(mine)
    def _():
        out_ref[...] = relayed_ref[...]

    @pl.when(jnp.logical_not(mine))
    def _():
        out_ref[...] = far_ref[...]


def pick(far, relayed, role):
    vmem = pl.BlockSpec(memory_space=pltpu.VMEM)
    return pl.pallas_call(
        lambda *refs: pick_kernel(role, *refs),
        out_shape=jax.ShapeDtypeStruct(far.shape, far.dtype),
        in_specs=[vmem, vmem],
        out_specs=vmem,
        compiler_params=pltpu.CompilerParams(vmem_limit_bytes=4 * MIB),
        name="pick",
    )(far, relayed)


def fetch_partners(block, count, hour):
    mirrored = hour % 2 == 1
    if count % LEVEL:
        way = -1 if mirrored else 1
        return [shift(block, count, way * steps) for steps in range(1, ROUNDS + 1)]
    near = send(block, count, mirrored, (0, 1, 0), (2, 3, 0), (1, 0, 1), (3, 2, 1))
    far = send(block, count, mirrored, (0, 2, 0), (1, 3, 0), (2, 1, 1))
    relayed = send(near, count, mirrored, (2, 0, 0))
    far = pick(far, relayed, LEVEL - 1 if mirrored else 0)
    other = send(far, count, mirrored, (0, 1, 0), (1, 0, 0), (2, 3, 0), (3, 2, 0))
    return [near, far, other]


def distances_of(mirrored):
    count = lax.axis_size("sta")
    if count % LEVEL:
        return list(range(1, ROUNDS + 1))
    role = lax.rem(lax.axis_index("sta"), LEVEL)
    role = LEVEL - 1 - role if mirrored else role
    chosen = []
    for q in range(ROUNDS):
        away = jnp.int32(DISTANCES[LEVEL - 1][q])
        for r in range(LEVEL - 1):
            away = jnp.where(role == r, DISTANCES[r][q], away)
        chosen.append(away)
    return chosen


def spectra(records, counts, gap_mask):
    channels, _, samples = records.shape
    hours = counts.shape[1]
    bins = samples // 2
    count = lax.axis_size("sta")
    table = fourier_matrix(samples)
    first, rest, valid, table = whiten_first(records, counts, gap_mask, table)
    whitened = [first] + [whiten_hour(rest, valid, table, hour) for hour in range(1, hours)]
    partners = [fetch_partners(whitened[hour], count, hour) for hour in range(hours)]
    sums = [None, None]
    for hour in range(hours):
        mirrored = hour % 2
        sums[mirrored] = pair_hour(
            [whitened[hour], *partners[hour]],
            sums[mirrored],
            hours,
            hour + 2 >= hours,
            mirrored == 1,
        )
    (behind, *back), (ahead, *forth) = sums
    from_ahead, from_rear = [], []
    for d in range(1, ROUNDS + 1):
        from_ahead.append(shift(back[d - 1], count, -d))
        from_rear.append(shift(forth[d - 1], count, d))
    stacked = join(behind, ahead, from_ahead, from_rear)
    stacked = stacked.reshape(2 * ROUNDS + 1, channels, channels, 2, bins)
    return jnp.transpose(stacked, (0, 3, 1, 2, 4))


def solution(mesh):
    in_specs = (P(("days", "sta"), None, None), P(("days", "sta"), None), P(("days", "sta"), None))
    out_specs = P(None, None, ("days", "sta"), None, None)
    return jax.shard_map(
        spectra, mesh=mesh, in_specs=in_specs, out_specs=out_specs, check_vma=False
    )
```

profile of v0, /device:TPU:0, one launch (start us, length us, event | category | flops | bytes accessed | tf_op | source)
XLA Modules:
  0.0 72.1 jit_solution(58701516391667729)
XLA Ops:
  0.0 1.7 %whiten_first.1 = (bf16[12,128,128]{2,1,0:T(8,128)(2,1)S(1)}, bf16[3,12,64,256]{3,2,1,0:T(8,128)(2,1)S(1)}, f32[4,4,128]{2,1,0:T(4,128)S(1)}, bf16[256,256]{1,0:T(8,128)(2,1)S(1)}) custom-call(s32[4,4]{1,0:T(4,128)} %counts_hbm.1, bf16[12,256,256]{2,1,0:T(8,128)(2,1)} %records_hbm.1, s32[4,256]{1,0:T(4,128)} %gap_hbm.1, bf16[256,256]{1,0:T(8,128)(2,1)} %constant.2.clone.table_hbm), custom_call_target="tpu_custom_call" | custom-call | flops 2000000000 | bytes 8000000 | tf_op jit(solution)/shard_map/whiten_first/pallas_call | solution.py:128
  2.2 1.3 %collective-permute-start.1 = (bf16[12,128,128]{2,1,0:T(8,128)(2,1)S(1)}, bf16[12,128,128]{2,1,0:T(8,128)(2,1)S(1)}, u32[]{:S(2)}, u32[]{:S(2)}) collective-permute-start(bf16[12,128,128]{2,1,0:T(8,128)(2,1)S(1)} %whiten_hour.3.refs_0_), channel_id=1, source_target_pairs={{15,13},{11,9},{7,5},{3,1},{14,12},{10,8},{6,4},{2,0},{13,10},{9,6... | collective-permute-start | bytes 1179656 | tf_op jit(solution)/shard_map/ppermute | solution.py:370
  4.0 6.9 %collective-permute-start.4 = (bf16[12,128,128]{2,1,0:T(8,128)(2,1)S(1)}, bf16[12,128,128]{2,1,0:T(8,128)(2,1)S(1)}, u32[]{:S(2)}, u32[]{:S(2)}) collective-permute-start(bf16[12,128,128]{2,1,0:T(8,128)(2,1)S(1)} %whiten_hour.4.refs_0_), channel_id=1, source_target_pairs={{15,14},{11,10},{7,6},{3,2},{13,12},{9,8},{5,4},{1,0},{14,11},{10,... | collective-permute-start | bytes 1179656 | tf_op jit(solution)/shard_map/ppermute | solution.py:370
  10.9 1.3 %collective-permute-start.5 = (bf16[12,128,128]{2,1,0:T(8,128)(2,1)S(1)}, bf16[12,128,128]{2,1,0:T(8,128)(2,1)S(1)}, u32[]{:S(2)}, u32[]{:S(2)}) collective-permute-start(bf16[12,128,128]{2,1,0:T(8,128)(2,1)S(1)} %whiten_hour.4.refs_0_), channel_id=1, source_target_pairs={{15,13},{11,9},{7,5},{3,1},{14,12},{10,8},{6,4},{2,0},{13,10},{9,6... | collective-permute-start | bytes 1179656 | tf_op jit(solution)/shard_map/ppermute | solution.py:370
  12.7 1.6 %collective-permute-start.8 = (bf16[12,128,128]{2,1,0:T(8,128)(2,1)S(1)}, bf16[12,128,128]{2,1,0:T(8,128)(2,1)S(1)}, u32[]{:S(2)}, u32[]{:S(2)}) collective-permute-start(bf16[12,128,128]{2,1,0:T(8,128)(2,1)S(1)} %whiten_hour.5.refs_0_), channel_id=1, source_target_pairs={{0,1},{4,5},{8,9},{12,13},{2,3},{6,7},{10,11},{14,15},{1,4},{5,8},... | collective-permute-start | bytes 1179656 | tf_op jit(solution)/shard_map/ppermute | solution.py:370
  14.4 1.2 %collective-permute-done.1.refs_0_ = bf16[12,128,128]{2,1,0:T(8,128)(2,1)S(1)} collective-permute-done((bf16[12,128,128]{2,1,0:T(8,128)(2,1)S(1)}, bf16[12,128,128]{2,1,0:T(8,128)(2,1)S(1)}, u32[]{:S(2)}, u32[]{:S(2)}) %collective-permute-start.1) | collective-permute-done | bytes 393248 | tf_op jit(solution)/shard_map/ppermute | solution.py:370
  15.6 2.3 %collective-permute-start.12 = (bf16[12,128,128]{2,1,0:T(8,128)(2,1)S(1)}, bf16[12,128,128]{2,1,0:T(8,128)(2,1)S(1)}, u32[]{:S(2)}, u32[]{:S(2)}) collective-permute-start(bf16[12,128,128]{2,1,0:T(8,128)(2,1)S(1)} %get-tuple-element.21.refs_0_), channel_id=1, source_target_pairs={{0,1},{4,5},{8,9},{12,13},{2,3},{6,7},{10,11},{14,15},{1,4},{5,8},... | collective-permute-start | bytes 1179656 | tf_op jit(solution)/shard_map/ppermute | solution.py:370
  17.9 2.6 %collective-permute-done.4.refs_1_ = bf16[12,128,128]{2,1,0:T(8,128)(2,1)S(1)} collective-permute-done((bf16[12,128,128]{2,1,0:T(8,128)(2,1)S(1)}, bf16[12,128,128]{2,1,0:T(8,128)(2,1)S(1)}, u32[]{:S(2)}, u32[]{:S(2)}) %collective-permute-start.4) | collective-permute-done | bytes 393248 | tf_op jit(solution)/shard_map/ppermute | solution.py:370
  20.5 0.7 collective-permute-start.6
  21.1 7.7 %collective-permute-done.refs_1_ = bf16[12,128,128]{2,1,0:T(8,128)(2,1)S(1)} collective-permute-done((bf16[12,128,128]{2,1,0:T(8,128)(2,1)S(1)}, bf16[12,128,128]{2,1,0:T(8,128)(2,1)S(1)}, u32[]{:S(2)}, u32[]{:S(2)}) %collective-permute-start) | collective-permute-done | bytes 393248 | tf_op jit(solution)/shard_map/ppermute | solution.py:370
  28.9 0.7 collective-permute-start.2
  29.6 1.3 %collective-permute-start.9 = (bf16[12,128,128]{2,1,0:T(8,128)(2,1)S(1)}, bf16[12,128,128]{2,1,0:T(8,128)(2,1)S(1)}, u32[]{:S(2)}, u32[]{:S(2)}) collective-permute-start(bf16[12,128,128]{2,1,0:T(8,128)(2,1)S(1)} %whiten_hour.5.refs_0_), channel_id=1, source_target_pairs={{0,2},{4,6},{8,10},{12,14},{1,3},{5,7},{9,11},{13,15},{2,5},{6,9},... | collective-permute-start | bytes 1179656 | tf_op jit(solution)/shard_map/ppermute | solution.py:370
  30.9 1.7 %collective-permute-done.8.refs_1_ = bf16[12,128,128]{2,1,0:T(8,128)(2,1)S(1)} collective-permute-done((bf16[12,128,128]{2,1,0:T(8,128)(2,1)S(1)}, bf16[12,128,128]{2,1,0:T(8,128)(2,1)S(1)}, u32[]{:S(2)}, u32[]{:S(2)}) %collective-permute-start.8) | collective-permute-done | bytes 393248 | tf_op jit(solution)/shard_map/ppermute | solution.py:370
  32.6 1.3 %collective-permute-start.10 = (bf16[12,128,128]{2,1,0:T(8,128)(2,1)S(1)}, bf16[12,128,128]{2,1,0:T(8,128)(2,1)S(1)}, u32[]{:S(2)}, u32[]{:S(2)}) collective-permute-start(bf16[12,128,128]{2,1,0:T(8,128)(2,1)S(1)} %collective-permute-done.8.refs_1_), channel_id=1, source_target_pairs={{2,0},{6,4},{10,8},{14,12},{18,16},{22,20},{26,24},{30,28}} | collective-permute-start | bytes 1179656 | tf_op jit(solution)/shard_map/ppermute | solution.py:370
  33.9 2.9 %collective-permute-done.12.refs_1_ = bf16[12,128,128]{2,1,0:T(8,128)(2,1)S(1)} collective-permute-done((bf16[12,128,128]{2,1,0:T(8,128)(2,1)S(1)}, bf16[12,128,128]{2,1,0:T(8,128)(2,1)S(1)}, u32[]{:S(2)}, u32[]{:S(2)}) %collective-permute-start.12) | collective-permute-done | bytes 393248 | tf_op jit(solution)/shard_map/ppermute | solution.py:370
  36.8 1.7 %collective-permute-start.13 = (bf16[12,128,128]{2,1,0:T(8,128)(2,1)S(1)}, bf16[12,128,128]{2,1,0:T(8,128)(2,1)S(1)}, u32[]{:S(2)}, u32[]{:S(2)}) collective-permute-start(bf16[12,128,128]{2,1,0:T(8,128)(2,1)S(1)} %get-tuple-element.21.refs_0_), channel_id=1, source_target_pairs={{0,2},{4,6},{8,10},{12,14},{1,3},{5,7},{9,11},{13,15},{2,5},{6,9},... | collective-permute-start | bytes 1179656 | tf_op jit(solution)/shard_map/ppermute | solution.py:370
  38.5 1.3 %collective-permute-start.14 = (bf16[12,128,128]{2,1,0:T(8,128)(2,1)S(1)}, bf16[12,128,128]{2,1,0:T(8,128)(2,1)S(1)}, u32[]{:S(2)}, u32[]{:S(2)}) collective-permute-start(bf16[12,128,128]{2,1,0:T(8,128)(2,1)S(1)} %collective-permute-done.12.refs_1_), channel_id=1, source_target_pairs={{2,0},{6,4},{10,8},{14,12},{18,16},{22,20},{26,24},{30,28}} | collective-permute-start | bytes 1179656 | tf_op jit(solution)/shard_map/ppermute | solution.py:370
  40.4 0.9 %collective-permute-start.3 = (bf16[12,128,128]{2,1,0:T(8,128)(2,1)S(1)}, bf16[12,128,128]{2,1,0:T(8,128)(2,1)S(1)}, u32[]{:S(2)}, u32[]{:S(2)}) collective-permute-start(bf16[12,128,128]{2,1,0:T(8,128)(2,1)S(1)} %pick.4.refs_2_), channel_id=1, source_target_pairs={{15,14},{11,10},{7,6},{3,2},{14,15},{10,11},{6,7},{2,3},{13,12},{9... | collective-permute-start | bytes 1179656 | tf_op jit(solution)/shard_map/ppermute | solution.py:370
  41.2 2.7 %collective-permute-done.10.refs_1_ = bf16[12,128,128]{2,1,0:T(8,128)(2,1)S(1)} collective-permute-done((bf16[12,128,128]{2,1,0:T(8,128)(2,1)S(1)}, bf16[12,128,128]{2,1,0:T(8,128)(2,1)S(1)}, u32[]{:S(2)}, u32[]{:S(2)}) %collective-permute-start.10) | collective-permute-done | bytes 393248 | tf_op jit(solution)/shard_map/ppermute | solution.py:370
  44.1 4.7 %collective-permute-done.13.refs_0_ = bf16[12,128,128]{2,1,0:T(8,128)(2,1)S(1)} collective-permute-done((bf16[12,128,128]{2,1,0:T(8,128)(2,1)S(1)}, bf16[12,128,128]{2,1,0:T(8,128)(2,1)S(1)}, u32[]{:S(2)}, u32[]{:S(2)}) %collective-permute-start.13) | collective-permute-done | bytes 393248 | tf_op jit(solution)/shard_map/ppermute | solution.py:370
  48.8 3.6 %collective-permute-done.14.refs_1_ = bf16[12,128,128]{2,1,0:T(8,128)(2,1)S(1)} collective-permute-done((bf16[12,128,128]{2,1,0:T(8,128)(2,1)S(1)}, bf16[12,128,128]{2,1,0:T(8,128)(2,1)S(1)}, u32[]{:S(2)}, u32[]{:S(2)}) %collective-permute-start.14) | collective-permute-done | bytes 393248 | tf_op jit(solution)/shard_map/ppermute | solution.py:370
  52.5 1.6 %pair_hour.2.refs_4_ = f32[2048,128]{1,0:T(8,128)S(1)} custom-call(bf16[12,128,128]{2,1,0:T(8,128)(2,1)S(1)} %whiten_hour.4.refs_0_, bf16[12,128,128]{2,1,0:T(8,128)(2,1)S(1)} %collective-permute-done.4.refs_1_, bf16[12,128,128]{2,1,0:T(8,128)(2,1)S(1)} %pick.5.refs_2_, bf16[12,128,128]{2,1,0:T(8,128)(2,1)S(1)} %collective-permute-done.7.refs_3_), custom_call_target="tpu_custom_call" | custom-call | flops 3000000000 | bytes 12000000 | tf_op jit(solution)/shard_map/pair_hour/pallas_call | solution.py:301
  54.1 2.4 %pair_hour_last.2 = (f32[4,288,128]{2,1,0:T(8,128)S(1)}, bf16[288,128]{1,0:T(8,128)(2,1)S(1)}, bf16[288,128]{1,0:T(8,128)(2,1)S(1)}, bf16[288,128]{1,0:T(8,128)(2,1)S(1)}) custom-call(bf16[12,128,128]{2,1,0:T(8,128)(2,1)S(1)} %whiten_hour.3.refs_0_, bf16[12,128,128]{2,1,0:T(8,128)(2,1)S(1)} %collective-permute-done.refs_1_, ...), custom_call_target="tpu_custom_call" | custom-call | flops 3000000000 | bytes 12000000 | tf_op jit(solution)/shard_map/pair_hour_last/pallas_call | solution.py:301
  57.1 1.1 %collective-permute-start.21 = (bf16[288,128]{1,0:T(8,128)(2,1)S(1)}, bf16[288,128]{1,0:T(8,128)(2,1)S(1)}, u32[]{:S(2)}, u32[]{:S(2)}) collective-permute-start(bf16[288,128]{1,0:T(8,128)(2,1)S(1)} %get-tuple-element.28), channel_id=1, source_target_pairs={{0,3},{1,4},{2,5},{3,6},{4,7},{5,8},{6,9},{7,10},{8,11},{9,12},{10... | collective-permute-start | bytes 221192 | tf_op jit(solution)/shard_map/ppermute | solution.py:375
  58.2 1.6 %pair_hour.3.refs_4_ = f32[2048,128]{1,0:T(8,128)S(1)} custom-call(bf16[12,128,128]{2,1,0:T(8,128)(2,1)S(1)} %get-tuple-element.21.refs_0_, bf16[12,128,128]{2,1,0:T(8,128)(2,1)S(1)} %collective-permute-done.12.refs_1_, bf16[12,128,128]{2,1,0:T(8,128)(2,1)S(1)} %pick.7.refs_2_, bf16[12,128,128]{2,1,0:T(8,128)(2,1)S(1)} %collective-permute-done.15.refs_3_), custom_call_target="tpu_custom_call" | custom-call | flops 3000000000 | bytes 12000000 | tf_op jit(solution)/shard_map/pair_hour/pallas_call | solution.py:301
  59.7 2.5 %pair_hour_last.3 = (f32[4,288,128]{2,1,0:T(8,128)S(1)}, bf16[288,128]{1,0:T(8,128)(2,1)S(1)}, bf16[288,128]{1,0:T(8,128)(2,1)S(1)}, bf16[288,128]{1,0:T(8,128)(2,1)S(1)}) custom-call(bf16[12,128,128]{2,1,0:T(8,128)(2,1)S(1)} %whiten_hour.5.refs_0_, bf16[12,128,128]{2,1,0:T(8,128)(2,1)S(1)} %collective-permute-done.8.refs_1_, ...), custom_call_target="tpu_custom_call" | custom-call | flops 3000000000 | bytes 12000000 | tf_op jit(solution)/shard_map/pair_hour_last/pallas_call | solution.py:301
  62.2 3.4 %collective-permute-start.16 = (bf16[288,128]{1,0:T(8,128)(2,1)S(1)}, bf16[288,128]{1,0:T(8,128)(2,1)S(1)}, u32[]{:S(2)}, u32[]{:S(2)}) collective-permute-start(bf16[288,128]{1,0:T(8,128)(2,1)S(1)} %get-tuple-element.22), channel_id=1, source_target_pairs={{0,15},{1,0},{2,1},{3,2},{4,3},{5,4},{6,5},{7,6},{8,7},{9,8},{10,9... | collective-permute-start | bytes 221192 | tf_op jit(solution)/shard_map/ppermute | solution.py:375
  65.5 1.9 %collective-permute-start.17 = (bf16[288,128]{1,0:T(8,128)(2,1)S(1)}, bf16[288,128]{1,0:T(8,128)(2,1)S(1)}, u32[]{:S(2)}, u32[]{:S(2)}) collective-permute-start(bf16[288,128]{1,0:T(8,128)(2,1)S(1)} %get-tuple-element.23), channel_id=1, source_target_pairs={{0,14},{1,15},{2,0},{3,1},{4,2},{5,3},{6,4},{7,5},{8,6},{9,7},{10,... | collective-permute-start | bytes 221192 | tf_op jit(solution)/shard_map/ppermute | solution.py:375
  67.5 1.3 %collective-permute-start.18 = (bf16[288,128]{1,0:T(8,128)(2,1)S(1)}, bf16[288,128]{1,0:T(8,128)(2,1)S(1)}, u32[]{:S(2)}, u32[]{:S(2)}) collective-permute-start(bf16[288,128]{1,0:T(8,128)(2,1)S(1)} %get-tuple-element.24), channel_id=1, source_target_pairs={{0,13},{1,14},{2,15},{3,0},{4,1},{5,2},{6,3},{7,4},{8,5},{9,6},{10... | collective-permute-start | bytes 221192 | tf_op jit(solution)/shard_map/ppermute | solution.py:375
  68.8 0.9 %join_below.1.refs_3_ = bf16[7,144,2,128]{3,2,1,0:T(2,128)(2,1)} custom-call(f32[4,288,128]{2,1,0:T(8,128)S(1)} %get-tuple-element.25.behind_ref, f32[4,288,128]{2,1,0:T(8,128)S(1)} %get-tuple-element.20.ahead_ref, bf16[288,128]{1,0:T(8,128)(2,1)S(1)} %collective-permute-done.19.refs_0_, bf16[288,128]{1,0:T(8,128)(2,1)S(1)} %collective-permute-done.20.refs_1_, ...), custom_call_target="tpu_custom_call" | custom-call | tf_op jit(solution)/shard_map/join_below/pallas_call | solution.py:336
  69.9 1.3 %collective-permute-done.18.refs_2_ = bf16[288,128]{1,0:T(8,128)(2,1)S(1)} collective-permute-done((bf16[288,128]{1,0:T(8,128)(2,1)S(1)}, bf16[288,128]{1,0:T(8,128)(2,1)S(1)}, u32[]{:S(2)}, u32[]{:S(2)}) %collective-permute-start.18) | collective-permute-done | bytes 73760 | tf_op jit(solution)/shard_map/ppermute | solution.py:375
  71.2 0.9 %join_above.1 = bf16[7,144,2,128]{3,2,1,0:T(2,128)(2,1)} custom-call(f32[4,288,128]{2,1,0:T(8,128)S(1)} %get-tuple-element.20.ahead_ref, bf16[288,128]{1,0:T(8,128)(2,1)S(1)} %collective-permute-done.16.refs_0_, bf16[288,128]{1,0:T(8,128)(2,1)S(1)} %collective-permute-done.17.refs_1_, ...), custom_call_target="tpu_custom_call", output_to_operand_aliasing={{}: (4, {})} | custom-call | tf_op jit(solution)/shard_map/join_above/pallas_call | solution.py:345
  (26 shorter events, 3.1 us)
Async XLA Ops:
  2.2 13.4 %collective-permute-start.1 = (bf16[12,128,128]{2,1,0:T(8,128)(2,1)S(1)}, bf16[12,128,128]{2,1,0:T(8,128)(2,1)S(1)}, u32[]{:S(2)}, u32[]{:S(2)}) collective-permute-start(bf16[12,128,128]{2,1,0:T(8,128)(2,1)S(1)} %whiten_hour.3.refs_0_), channel_id=1, source_target_pairs={{15,13},{11,9},{7,5},{3,1},{14,12},{10,8},{6,4},{2,0},{13,10},{9,6... | collective-permute-start | bytes 1179656 | tf_op jit(solution)/shard_map/ppermute | solution.py:370
  4.0 16.5 %collective-permute-start.4 = (bf16[12,128,128]{2,1,0:T(8,128)(2,1)S(1)}, bf16[12,128,128]{2,1,0:T(8,128)(2,1)S(1)}, u32[]{:S(2)}, u32[]{:S(2)}) collective-permute-start(bf16[12,128,128]{2,1,0:T(8,128)(2,1)S(1)} %whiten_hour.4.refs_0_), channel_id=1, source_target_pairs={{15,14},{11,10},{7,6},{3,2},{13,12},{9,8},{5,4},{1,0},{14,11},{10,... | collective-permute-start | bytes 1179656 | tf_op jit(solution)/shard_map/ppermute | solution.py:370
  10.9 18.0 %collective-permute-start = (bf16[12,128,128]{2,1,0:T(8,128)(2,1)S(1)}, bf16[12,128,128]{2,1,0:T(8,128)(2,1)S(1)}, u32[]{:S(2)}, u32[]{:S(2)}) collective-permute-start(bf16[12,128,128]{2,1,0:T(8,128)(2,1)S(1)} %whiten_hour.3.refs_0_), channel_id=1, source_target_pairs={{15,14},{11,10},{7,6},{3,2},{13,12},{9,8},{5,4},{1,0},{14,11},{10,... | collective-permute-start | bytes 1179656 | tf_op jit(solution)/shard_map/ppermute | solution.py:370
  10.9 18.6 %collective-permute-start.5 = (bf16[12,128,128]{2,1,0:T(8,128)(2,1)S(1)}, bf16[12,128,128]{2,1,0:T(8,128)(2,1)S(1)}, u32[]{:S(2)}, u32[]{:S(2)}) collective-permute-start(bf16[12,128,128]{2,1,0:T(8,128)(2,1)S(1)} %whiten_hour.4.refs_0_), channel_id=1, source_target_pairs={{15,13},{11,9},{7,5},{3,1},{14,12},{10,8},{6,4},{2,0},{13,10},{9,6... | collective-permute-start | bytes 1179656 | tf_op jit(solution)/shard_map/ppermute | solution.py:370
  12.7 19.9 %collective-permute-start.8 = (bf16[12,128,128]{2,1,0:T(8,128)(2,1)S(1)}, bf16[12,128,128]{2,1,0:T(8,128)(2,1)S(1)}, u32[]{:S(2)}, u32[]{:S(2)}) collective-permute-start(bf16[12,128,128]{2,1,0:T(8,128)(2,1)S(1)} %whiten_hour.5.refs_0_), channel_id=1, source_target_pairs={{0,1},{4,5},{8,9},{12,13},{2,3},{6,7},{10,11},{14,15},{1,4},{5,8},... | collective-permute-start | bytes 1179656 | tf_op jit(solution)/shard_map/ppermute | solution.py:370
  15.6 21.2 %collective-permute-start.12 = (bf16[12,128,128]{2,1,0:T(8,128)(2,1)S(1)}, bf16[12,128,128]{2,1,0:T(8,128)(2,1)S(1)}, u32[]{:S(2)}, u32[]{:S(2)}) collective-permute-start(bf16[12,128,128]{2,1,0:T(8,128)(2,1)S(1)} %get-tuple-element.21.refs_0_), channel_id=1, source_target_pairs={{0,1},{4,5},{8,9},{12,13},{2,3},{6,7},{10,11},{14,15},{1,4},{5,8},... | collective-permute-start | bytes 1179656 | tf_op jit(solution)/shard_map/ppermute | solution.py:370
  20.5 18.0 %collective-permute-start.6 = (bf16[12,128,128]{2,1,0:T(8,128)(2,1)S(1)}, bf16[12,128,128]{2,1,0:T(8,128)(2,1)S(1)}, u32[]{:S(2)}, u32[]{:S(2)}) collective-permute-start(bf16[12,128,128]{2,1,0:T(8,128)(2,1)S(1)} %collective-permute-done.4.refs_1_), channel_id=1, source_target_pairs={{13,15},{9,11},{5,7},{1,3},{29,31},{25,27},{21,23},{17,19}} | collective-permute-start | bytes 1179656 | tf_op jit(solution)/shard_map/ppermute | solution.py:370
  28.9 11.0 %collective-permute-start.2 = (bf16[12,128,128]{2,1,0:T(8,128)(2,1)S(1)}, bf16[12,128,128]{2,1,0:T(8,128)(2,1)S(1)}, u32[]{:S(2)}, u32[]{:S(2)}) collective-permute-start(bf16[12,128,128]{2,1,0:T(8,128)(2,1)S(1)} %collective-permute-done.refs_1_), channel_id=1, source_target_pairs={{13,15},{9,11},{5,7},{1,3},{29,31},{25,27},{21,23},{17,19}} | collective-permute-start | bytes 1179656 | tf_op jit(solution)/shard_map/ppermute | solution.py:370
  29.6 10.8 %collective-permute-start.9 = (bf16[12,128,128]{2,1,0:T(8,128)(2,1)S(1)}, bf16[12,128,128]{2,1,0:T(8,128)(2,1)S(1)}, u32[]{:S(2)}, u32[]{:S(2)}) collective-permute-start(bf16[12,128,128]{2,1,0:T(8,128)(2,1)S(1)} %whiten_hour.5.refs_0_), channel_id=1, source_target_pairs={{0,2},{4,6},{8,10},{12,14},{1,3},{5,7},{9,11},{13,15},{2,5},{6,9},... | collective-permute-start | bytes 1179656 | tf_op jit(solution)/shard_map/ppermute | solution.py:370
  32.6 11.4 %collective-permute-start.10 = (bf16[12,128,128]{2,1,0:T(8,128)(2,1)S(1)}, bf16[12,128,128]{2,1,0:T(8,128)(2,1)S(1)}, u32[]{:S(2)}, u32[]{:S(2)}) collective-permute-start(bf16[12,128,128]{2,1,0:T(8,128)(2,1)S(1)} %collective-permute-done.8.refs_1_), channel_id=1, source_target_pairs={{2,0},{6,4},{10,8},{14,12},{18,16},{22,20},{26,24},{30,28}} | collective-permute-start | bytes 1179656 | tf_op jit(solution)/shard_map/ppermute | solution.py:370
  36.8 12.0 %collective-permute-start.13 = (bf16[12,128,128]{2,1,0:T(8,128)(2,1)S(1)}, bf16[12,128,128]{2,1,0:T(8,128)(2,1)S(1)}, u32[]{:S(2)}, u32[]{:S(2)}) collective-permute-start(bf16[12,128,128]{2,1,0:T(8,128)(2,1)S(1)} %get-tuple-element.21.refs_0_), channel_id=1, source_target_pairs={{0,2},{4,6},{8,10},{12,14},{1,3},{5,7},{9,11},{13,15},{2,5},{6,9},... | collective-permute-start | bytes 1179656 | tf_op jit(solution)/shard_map/ppermute | solution.py:370
  38.5 13.9 %collective-permute-start.14 = (bf16[12,128,128]{2,1,0:T(8,128)(2,1)S(1)}, bf16[12,128,128]{2,1,0:T(8,128)(2,1)S(1)}, u32[]{:S(2)}, u32[]{:S(2)}) collective-permute-start(bf16[12,128,128]{2,1,0:T(8,128)(2,1)S(1)} %collective-permute-done.12.refs_1_), channel_id=1, source_target_pairs={{2,0},{6,4},{10,8},{14,12},{18,16},{22,20},{26,24},{30,28}} | collective-permute-start | bytes 1179656 | tf_op jit(solution)/shard_map/ppermute | solution.py:370
  39.9 12.6 %collective-permute-start.7 = (bf16[12,128,128]{2,1,0:T(8,128)(2,1)S(1)}, bf16[12,128,128]{2,1,0:T(8,128)(2,1)S(1)}, u32[]{:S(2)}, u32[]{:S(2)}) collective-permute-start(bf16[12,128,128]{2,1,0:T(8,128)(2,1)S(1)} %pick.5.refs_2_), channel_id=1, source_target_pairs={{15,14},{11,10},{7,6},{3,2},{14,15},{10,11},{6,7},{2,3},{13,12},{9... | collective-permute-start | bytes 1179656 | tf_op jit(solution)/shard_map/ppermute | solution.py:370
  40.4 13.7 %collective-permute-start.3 = (bf16[12,128,128]{2,1,0:T(8,128)(2,1)S(1)}, bf16[12,128,128]{2,1,0:T(8,128)(2,1)S(1)}, u32[]{:S(2)}, u32[]{:S(2)}) collective-permute-start(bf16[12,128,128]{2,1,0:T(8,128)(2,1)S(1)} %pick.4.refs_2_), channel_id=1, source_target_pairs={{15,14},{11,10},{7,6},{3,2},{14,15},{10,11},{6,7},{2,3},{13,12},{9... | collective-permute-start | bytes 1179656 | tf_op jit(solution)/shard_map/ppermute | solution.py:370
  44.0 15.7 %collective-permute-start.11 = (bf16[12,128,128]{2,1,0:T(8,128)(2,1)S(1)}, bf16[12,128,128]{2,1,0:T(8,128)(2,1)S(1)}, u32[]{:S(2)}, u32[]{:S(2)}) collective-permute-start(bf16[12,128,128]{2,1,0:T(8,128)(2,1)S(1)} %pick.6.refs_2_), channel_id=1, source_target_pairs={{0,1},{4,5},{8,9},{12,13},{1,0},{5,4},{9,8},{13,12},{2,3},{6,7},{1... | collective-permute-start | bytes 1179656 | tf_op jit(solution)/shard_map/ppermute | solution.py:370
  52.4 5.8 %collective-permute-start.15 = (bf16[12,128,128]{2,1,0:T(8,128)(2,1)S(1)}, bf16[12,128,128]{2,1,0:T(8,128)(2,1)S(1)}, u32[]{:S(2)}, u32[]{:S(2)}) collective-permute-start(bf16[12,128,128]{2,1,0:T(8,128)(2,1)S(1)} %pick.7.refs_2_), channel_id=1, source_target_pairs={{0,1},{4,5},{8,9},{12,13},{1,0},{5,4},{9,8},{13,12},{2,3},{6,7},{1... | collective-permute-start | bytes 1179656 | tf_op jit(solution)/shard_map/ppermute | solution.py:370
  56.5 10.9 %collective-permute-start.19 = (bf16[288,128]{1,0:T(8,128)(2,1)S(1)}, bf16[288,128]{1,0:T(8,128)(2,1)S(1)}, u32[]{:S(2)}, u32[]{:S(2)}) collective-permute-start(bf16[288,128]{1,0:T(8,128)(2,1)S(1)} %get-tuple-element.26), channel_id=1, source_target_pairs={{0,1},{1,2},{2,3},{3,4},{4,5},{5,6},{6,7},{7,8},{8,9},{9,10},{10,1... | collective-permute-start | bytes 221192 | tf_op jit(solution)/shard_map/ppermute | solution.py:375
  57.0 11.7 %collective-permute-start.20 = (bf16[288,128]{1,0:T(8,128)(2,1)S(1)}, bf16[288,128]{1,0:T(8,128)(2,1)S(1)}, u32[]{:S(2)}, u32[]{:S(2)}) collective-permute-start(bf16[288,128]{1,0:T(8,128)(2,1)S(1)} %get-tuple-element.27), channel_id=1, source_target_pairs={{0,2},{1,3},{2,4},{3,5},{4,6},{5,7},{6,8},{7,9},{8,10},{9,11},{10,... | collective-permute-start | bytes 221192 | tf_op jit(solution)/shard_map/ppermute | solution.py:375
  57.1 11.7 %collective-permute-start.21 = (bf16[288,128]{1,0:T(8,128)(2,1)S(1)}, bf16[288,128]{1,0:T(8,128)(2,1)S(1)}, u32[]{:S(2)}, u32[]{:S(2)}) collective-permute-start(bf16[288,128]{1,0:T(8,128)(2,1)S(1)} %get-tuple-element.28), channel_id=1, source_target_pairs={{0,3},{1,4},{2,5},{3,6},{4,7},{5,8},{6,9},{7,10},{8,11},{9,12},{10... | collective-permute-start | bytes 221192 | tf_op jit(solution)/shard_map/ppermute | solution.py:375
  62.2 7.5 %collective-permute-start.16 = (bf16[288,128]{1,0:T(8,128)(2,1)S(1)}, bf16[288,128]{1,0:T(8,128)(2,1)S(1)}, u32[]{:S(2)}, u32[]{:S(2)}) collective-permute-start(bf16[288,128]{1,0:T(8,128)(2,1)S(1)} %get-tuple-element.22), channel_id=1, source_target_pairs={{0,15},{1,0},{2,1},{3,2},{4,3},{5,4},{6,5},{7,6},{8,7},{9,8},{10,9... | collective-permute-start | bytes 221192 | tf_op jit(solution)/shard_map/ppermute | solution.py:375
  65.5 4.4 %collective-permute-start.17 = (bf16[288,128]{1,0:T(8,128)(2,1)S(1)}, bf16[288,128]{1,0:T(8,128)(2,1)S(1)}, u32[]{:S(2)}, u32[]{:S(2)}) collective-permute-start(bf16[288,128]{1,0:T(8,128)(2,1)S(1)} %get-tuple-element.23), channel_id=1, source_target_pairs={{0,14},{1,15},{2,0},{3,1},{4,2},{5,3},{6,4},{7,5},{8,6},{9,7},{10,... | collective-permute-start | bytes 221192 | tf_op jit(solution)/shard_map/ppermute | solution.py:375
  67.5 3.8 %collective-permute-start.18 = (bf16[288,128]{1,0:T(8,128)(2,1)S(1)}, bf16[288,128]{1,0:T(8,128)(2,1)S(1)}, u32[]{:S(2)}, u32[]{:S(2)}) collective-permute-start(bf16[288,128]{1,0:T(8,128)(2,1)S(1)} %get-tuple-element.24), channel_id=1, source_target_pairs={{0,13},{1,14},{2,15},{3,0},{4,1},{5,2},{6,3},{7,4},{8,5},{9,6},{10... | collective-permute-start | bytes 221192 | tf_op jit(solution)/shard_map/ppermute | solution.py:375
where the time goes:
time: 73.2 us; the launch traced here: 72.1 us
  starting transfers between devices  29.6 us (40%)
  waiting for transfers between devices  29.1 us (40%)
  Pallas kernels  13.1 us (18%)
    ppermute x16, waiting for transfers between devices, send(): return lax.ppermute(value, 'sta', pairs)  27.6 us
    ppermute x16, starting transfers between devices, send(): return lax.ppermute(value, 'sta', pairs)  21.4 us
    ppermute x6, starting transfers between devices, shift(): return lax.ppermute(value, 'sta', pairs)  8.21 us
    pallas_call x4, Pallas kernels, pair_hour(): pl.pallas_call(lambda *refs: pair_hour_kernel(hours, first, last, mirrore...  8.01 us
    pallas_call x1, Pallas kernels, whiten_first(): pl.pallas_call(whiten_first_kernel, out_shape=[jax.ShapeDtypeStruct((chan...  1.66 us
    ppermute x6, waiting for transfers between devices, shift(): return lax.ppermute(value, 'sta', pairs)  1.55 us
    pallas_call x3, Pallas kernels, whiten_hour(): pl.pallas_call(lambda *refs: whiten_hour_kernel(hour, *refs), out_shape=j...  1.52 us
  transfers between devices with their start and end apart: 22, of which 11 were waited for; matrix products, arithmetic and copies ran while one was open for 0% of the time, Pallas kernels for 14%

commit v1 on v0

--- a/solution.py
+++ b/solution.py
@@ -105,10 +105,12 @@
         pltpu.make_async_copy(source, target, sems.at[i])
         for i, (source, target) in enumerate(moves)
     ]
-    for copy in copies:
+    for copy in copies[:now]:
         copy.start()
     for copy in copies[:now]:
         copy.wait()
+    for copy in copies[now:]:
+        copy.start()
     valid = [validity_rows(hour, seg_hour, counts_ref, gap_ref) for hour in range(hours)]
     for hour in range(1, hours):
         for station, row in enumerate(valid[hour]):
@@ -375,39 +377,13 @@
     return lax.ppermute(value, "sta", pairs)
 
 
-def pick_kernel(role, far_ref, relayed_ref, out_ref):
-    mine = lax.rem(lax.axis_index("sta"), LEVEL) == role
-
-    @pl.when(mine)
-    def _():
-        out_ref[...] = relayed_ref[...]
-
-    @pl.when(jnp.logical_not(mine))
-    def _():
-        out_ref[...] = far_ref[...]
-
-
-def pick(far, relayed, role):
-    vmem = pl.BlockSpec(memory_space=pltpu.VMEM)
-    return pl.pallas_call(
-        lambda *refs: pick_kernel(role, *refs),
-        out_shape=jax.ShapeDtypeStruct(far.shape, far.dtype),
-        in_specs=[vmem, vmem],
-        out_specs=vmem,
-        compiler_params=pltpu.CompilerParams(vmem_limit_bytes=4 * MIB),
-        name="pick",
-    )(far, relayed)
-
-
 def fetch_partners(block, count, hour):
     mirrored = hour % 2 == 1
     if count % LEVEL:
         way = -1 if mirrored else 1
         return [shift(block, count, way * steps) for steps in range(1, ROUNDS + 1)]
+    far = send(block, count, mirrored, (0, 2, 0), (1, 3, 0), (2, 1, 1), (3, 0, 1))
     near = send(block, count, mirrored, (0, 1, 0), (2, 3, 0), (1, 0, 1), (3, 2, 1))
-    far = send(block, count, mirrored, (0, 2, 0), (1, 3, 0), (2, 1, 1))
-    relayed = send(near, count, mirrored, (2, 0, 0))
-    far = pick(far, relayed, LEVEL - 1 if mirrored else 0)
     other = send(far, count, mirrored, (0, 1, 0), (1, 0, 0), (2, 3, 0), (3, 2, 0))
     return [near, far, other]
 

time: 73.2 us -> 64.8 us (0.89); the launches traced: 72.1 us -> 64.4 us
  starting transfers between devices: 29.6 us -> 19.8 us
  waiting for transfers between devices: 29.1 us -> 30.6 us
  Pallas kernels: 13.1 us -> 14 us
    ppermute x16 -> x12, starting transfers between devices: 21.4 us -> 14.9 us  [send(): return lax.ppermute(value, 'sta', pairs)]
    ppermute x6, starting transfers between devices: 8.21 us -> 4.88 us  [shift(): return lax.ppermute(value, 'sta', pairs)]
    pallas_call x1, Pallas kernels: 1.66 us -> 2.68 us  [whiten_first(): pl.pallas_call(whiten_first_kernel, out_shape=[jax.ShapeDtypeStruct((chan...]
    ppermute x6, waiting for transfers between devices: 1.55 us -> 2.37 us  [shift(): return lax.ppermute(value, 'sta', pairs)]
    ppermute x16 -> x12, waiting for transfers between devices: 27.6 us -> 28.2 us  [send(): return lax.ppermute(value, 'sta', pairs)]
  transfers between devices with their start and end apart: 22 -> 18, of which waited for: 11 -> 7; matrix products, arithmetic and copies ran while one was open for 0% -> 0% of each run, Pallas kernels for 14% -> 15%
where the time goes in v1:
time: 64.8 us; the launch traced here: 64.4 us
  waiting for transfers between devices  30.6 us (47%)
  starting transfers between devices  19.8 us (31%)
  Pallas kernels  14 us (22%)
    ppermute x12, waiting for transfers between devices, send(): return lax.ppermute(value, 'sta', pairs)  28.2 us
    ppermute x12, starting transfers between devices, send(): return lax.ppermute(value, 'sta', pairs)  14.9 us
    pallas_call x4, Pallas kernels, pair_hour(): pl.pallas_call(lambda *refs: pair_hour_kernel(hours, first, last, mirrore...  7.97 us
    ppermute x6, starting transfers between devices, shift(): return lax.ppermute(value, 'sta', pairs)  4.88 us
    pallas_call x1, Pallas kernels, whiten_first(): pl.pallas_call(whiten_first_kernel, out_shape=[jax.ShapeDtypeStruct((chan...  2.68 us
    ppermute x6, waiting for transfers between devices, shift(): return lax.ppermute(value, 'sta', pairs)  2.37 us
    pallas_call x3, Pallas kernels, whiten_hour(): pl.pallas_call(lambda *refs: whiten_hour_kernel(hour, *refs), out_shape=j...  1.53 us
  transfers between devices with their start and end apart: 18, of which 7 were waited for; matrix products, arithmetic and copies ran while one was open for 0% of the time, Pallas kernels for 15%

profile of v1, /device:TPU:0, one launch (start us, length us, event | category | flops | bytes accessed | tf_op | source)
XLA Modules:
  0.0 64.4 jit_solution(2565843192445344987)
XLA Ops:
  0.0 2.7 %whiten_first.1 = (bf16[12,128,128]{2,1,0:T(8,128)(2,1)S(1)}, bf16[3,12,64,256]{3,2,1,0:T(8,128)(2,1)S(1)}, f32[4,4,128]{2,1,0:T(4,128)S(1)}, bf16[256,256]{1,0:T(8,128)(2,1)S(1)}) custom-call(s32[4,4]{1,0:T(4,128)} %counts_hbm.1, bf16[12,256,256]{2,1,0:T(8,128)(2,1)} %records_hbm.1, s32[4,256]{1,0:T(4,128)} %gap_hbm.1, bf16[256,256]{1,0:T(8,128)(2,1)} %constant.2.clone.table_hbm), custom_call_target="tpu_custom_call" | custom-call | flops 2000000000 | bytes 8000000 | tf_op jit(solution)/shard_map/whiten_first/pallas_call | solution.py:130
  2.7 0.5 whiten_hour.4.refs_0_
  3.2 5.5 %collective-permute-start.4 = (bf16[12,128,128]{2,1,0:T(8,128)(2,1)S(1)}, bf16[12,128,128]{2,1,0:T(8,128)(2,1)S(1)}, u32[]{:S(2)}, u32[]{:S(2)}) collective-permute-start(bf16[12,128,128]{2,1,0:T(8,128)(2,1)S(1)} %whiten_hour.4.refs_0_), channel_id=1, source_target_pairs={{15,13},{11,9},{7,5},{3,1},{14,12},{10,8},{6,4},{2,0},{13,10},{9,6... | collective-permute-start | bytes 1179656 | tf_op jit(solution)/shard_map/ppermute | solution.py:372
  8.7 0.5 whiten_hour.3.refs_0_
  9.3 4.5 %collective-permute-start.1 = (bf16[12,128,128]{2,1,0:T(8,128)(2,1)S(1)}, bf16[12,128,128]{2,1,0:T(8,128)(2,1)S(1)}, u32[]{:S(2)}, u32[]{:S(2)}) collective-permute-start(bf16[12,128,128]{2,1,0:T(8,128)(2,1)S(1)} %whiten_hour.3.refs_0_), channel_id=1, source_target_pairs={{15,13},{11,9},{7,5},{3,1},{14,12},{10,8},{6,4},{2,0},{13,10},{9,6... | collective-permute-start | bytes 1179656 | tf_op jit(solution)/shard_map/ppermute | solution.py:372
  13.8 0.0 collective-permute-start.3
  13.8 10.9 %collective-permute-done.4.refs_2_ = bf16[12,128,128]{2,1,0:T(8,128)(2,1)S(1)} collective-permute-done((bf16[12,128,128]{2,1,0:T(8,128)(2,1)S(1)}, bf16[12,128,128]{2,1,0:T(8,128)(2,1)S(1)}, u32[]{:S(2)}, u32[]{:S(2)}) %collective-permute-start.4) | collective-permute-done | bytes 393248 | tf_op jit(solution)/shard_map/ppermute | solution.py:372
  24.7 0.0 collective-permute-start.5
  24.7 0.5 whiten_hour.5.refs_0_
  25.2 0.1 collective-permute-start.7
  25.3 7.7 %collective-permute-done.10.refs_2_ = bf16[12,128,128]{2,1,0:T(8,128)(2,1)S(1)} collective-permute-done((bf16[12,128,128]{2,1,0:T(8,128)(2,1)S(1)}, bf16[12,128,128]{2,1,0:T(8,128)(2,1)S(1)}, u32[]{:S(2)}, u32[]{:S(2)}) %collective-permute-start.10) | collective-permute-done | bytes 393248 | tf_op jit(solution)/shard_map/ppermute | solution.py:372
  32.9 1.1 %collective-permute-start = (bf16[12,128,128]{2,1,0:T(8,128)(2,1)S(1)}, bf16[12,128,128]{2,1,0:T(8,128)(2,1)S(1)}, u32[]{:S(2)}, u32[]{:S(2)}) collective-permute-start(bf16[12,128,128]{2,1,0:T(8,128)(2,1)S(1)} %whiten_hour.3.refs_0_), channel_id=1, source_target_pairs={{15,14},{11,10},{7,6},{3,2},{13,12},{9,8},{5,4},{1,0},{14,11},{10,... | collective-permute-start | bytes 1179656 | tf_op jit(solution)/shard_map/ppermute | solution.py:372
  34.1 6.6 %collective-permute-done.1.refs_2_ = bf16[12,128,128]{2,1,0:T(8,128)(2,1)S(1)} collective-permute-done((bf16[12,128,128]{2,1,0:T(8,128)(2,1)S(1)}, bf16[12,128,128]{2,1,0:T(8,128)(2,1)S(1)}, u32[]{:S(2)}, u32[]{:S(2)}) %collective-permute-start.1) | collective-permute-done | bytes 393248 | tf_op jit(solution)/shard_map/ppermute | solution.py:372
  40.7 0.5 collective-permute-start.9
  41.2 1.4 %collective-permute-start.11 = (bf16[12,128,128]{2,1,0:T(8,128)(2,1)S(1)}, bf16[12,128,128]{2,1,0:T(8,128)(2,1)S(1)}, u32[]{:S(2)}, u32[]{:S(2)}) collective-permute-start(bf16[12,128,128]{2,1,0:T(8,128)(2,1)S(1)} %collective-permute-done.10.refs_2_), channel_id=1, source_target_pairs={{0,1},{4,5},{8,9},{12,13},{1,0},{5,4},{9,8},{13,12},{2,3},{6,7},{1... | collective-permute-start | bytes 1179656 | tf_op jit(solution)/shard_map/ppermute | solution.py:372
  42.6 1.6 %pair_hour.2.refs_4_ = f32[2048,128]{1,0:T(8,128)S(1)} custom-call(bf16[12,128,128]{2,1,0:T(8,128)(2,1)S(1)} %whiten_hour.4.refs_0_, bf16[12,128,128]{2,1,0:T(8,128)(2,1)S(1)} %collective-permute-done.3.refs_1_, bf16[12,128,128]{2,1,0:T(8,128)(2,1)S(1)} %collective-permute-done.4.refs_2_, bf16[12,128,128]{2,1,0:T(8,128)(2,1)S(1)} %collective-permute-done.5.refs_3_), custom_call_target="tpu_custom_call" | custom-call | flops 3000000000 | bytes 12000000 | tf_op jit(solution)/shard_map/pair_hour/pallas_call | solution.py:303
  44.1 0.1 collective-permute-start.6
  44.2 1.7 %collective-permute-start.8 = (bf16[12,128,128]{2,1,0:T(8,128)(2,1)S(1)}, bf16[12,128,128]{2,1,0:T(8,128)(2,1)S(1)}, u32[]{:S(2)}, u32[]{:S(2)}) collective-permute-start(bf16[12,128,128]{2,1,0:T(8,128)(2,1)S(1)} %collective-permute-done.7.refs_2_), channel_id=1, source_target_pairs={{0,1},{4,5},{8,9},{12,13},{1,0},{5,4},{9,8},{13,12},{2,3},{6,7},{1... | collective-permute-start | bytes 1179656 | tf_op jit(solution)/shard_map/ppermute | solution.py:372
  45.9 2.4 %pair_hour_last.2 = (f32[4,288,128]{2,1,0:T(8,128)S(1)}, bf16[288,128]{1,0:T(8,128)(2,1)S(1)}, bf16[288,128]{1,0:T(8,128)(2,1)S(1)}, bf16[288,128]{1,0:T(8,128)(2,1)S(1)}) custom-call(bf16[12,128,128]{2,1,0:T(8,128)(2,1)S(1)} %whiten_hour.3.refs_0_, bf16[12,128,128]{2,1,0:T(8,128)(2,1)S(1)} %collective-permute-done.refs_1_, ...), custom_call_target="tpu_custom_call" | custom-call | flops 3000000000 | bytes 12000000 | tf_op jit(solution)/shard_map/pair_hour_last/pallas_call | solution.py:303
  48.3 0.1 collective-permute-start.15
  48.4 1.5 %collective-permute-done.9.refs_1_ = bf16[12,128,128]{2,1,0:T(8,128)(2,1)S(1)} collective-permute-done((bf16[12,128,128]{2,1,0:T(8,128)(2,1)S(1)}, bf16[12,128,128]{2,1,0:T(8,128)(2,1)S(1)}, u32[]{:S(2)}, u32[]{:S(2)}) %collective-permute-start.9) | collective-permute-done | bytes 393248 | tf_op jit(solution)/shard_map/ppermute | solution.py:372
  50.0 1.1 %collective-permute-start.17 = (bf16[288,128]{1,0:T(8,128)(2,1)S(1)}, bf16[288,128]{1,0:T(8,128)(2,1)S(1)}, u32[]{:S(2)}, u32[]{:S(2)}) collective-permute-start(bf16[288,128]{1,0:T(8,128)(2,1)S(1)} %get-tuple-element.28), channel_id=1, source_target_pairs={{0,3},{1,4},{2,5},{3,6},{4,7},{5,8},{6,9},{7,10},{8,11},{9,12},{10... | collective-permute-start | bytes 221192 | tf_op jit(solution)/shard_map/ppermute | solution.py:377
  51.1 1.6 %pair_hour.3.refs_4_ = f32[2048,128]{1,0:T(8,128)S(1)} custom-call(bf16[12,128,128]{2,1,0:T(8,128)(2,1)S(1)} %get-tuple-element.21.refs_0_, bf16[12,128,128]{2,1,0:T(8,128)(2,1)S(1)} %collective-permute-done.9.refs_1_, bf16[12,128,128]{2,1,0:T(8,128)(2,1)S(1)} %collective-permute-done.10.refs_2_, bf16[12,128,128]{2,1,0:T(8,128)(2,1)S(1)} %collective-permute-done.11.refs_3_), custom_call_target="tpu_custom_call" | custom-call | flops 3000000000 | bytes 12000000 | tf_op jit(solution)/shard_map/pair_hour/pallas_call | solution.py:303
  52.7 1.5 %collective-permute-done.6.refs_1_ = bf16[12,128,128]{2,1,0:T(8,128)(2,1)S(1)} collective-permute-done((bf16[12,128,128]{2,1,0:T(8,128)(2,1)S(1)}, bf16[12,128,128]{2,1,0:T(8,128)(2,1)S(1)}, u32[]{:S(2)}, u32[]{:S(2)}) %collective-permute-start.6) | collective-permute-done | bytes 393248 | tf_op jit(solution)/shard_map/ppermute | solution.py:372
  54.2 2.4 %pair_hour_last.3 = (f32[4,288,128]{2,1,0:T(8,128)S(1)}, bf16[288,128]{1,0:T(8,128)(2,1)S(1)}, bf16[288,128]{1,0:T(8,128)(2,1)S(1)}, bf16[288,128]{1,0:T(8,128)(2,1)S(1)}) custom-call(bf16[12,128,128]{2,1,0:T(8,128)(2,1)S(1)} %whiten_hour.5.refs_0_, bf16[12,128,128]{2,1,0:T(8,128)(2,1)S(1)} %collective-permute-done.6.refs_1_, ...), custom_call_target="tpu_custom_call" | custom-call | flops 3000000000 | bytes 12000000 | tf_op jit(solution)/shard_map/pair_hour_last/pallas_call | solution.py:303
  56.6 1.8 %collective-permute-start.12 = (bf16[288,128]{1,0:T(8,128)(2,1)S(1)}, bf16[288,128]{1,0:T(8,128)(2,1)S(1)}, u32[]{:S(2)}, u32[]{:S(2)}) collective-permute-start(bf16[288,128]{1,0:T(8,128)(2,1)S(1)} %get-tuple-element.22), channel_id=1, source_target_pairs={{0,15},{1,0},{2,1},{3,2},{4,3},{5,4},{6,5},{7,6},{8,7},{9,8},{10,9... | collective-permute-start | bytes 221192 | tf_op jit(solution)/shard_map/ppermute | solution.py:377
  58.4 1.2 %collective-permute-start.13 = (bf16[288,128]{1,0:T(8,128)(2,1)S(1)}, bf16[288,128]{1,0:T(8,128)(2,1)S(1)}, u32[]{:S(2)}, u32[]{:S(2)}) collective-permute-start(bf16[288,128]{1,0:T(8,128)(2,1)S(1)} %get-tuple-element.23), channel_id=1, source_target_pairs={{0,14},{1,15},{2,0},{3,1},{4,2},{5,3},{6,4},{7,5},{8,6},{9,7},{10,... | collective-permute-start | bytes 221192 | tf_op jit(solution)/shard_map/ppermute | solution.py:377
  59.6 0.6 %collective-permute-start.14 = (bf16[288,128]{1,0:T(8,128)(2,1)S(1)}, bf16[288,128]{1,0:T(8,128)(2,1)S(1)}, u32[]{:S(2)}, u32[]{:S(2)}) collective-permute-start(bf16[288,128]{1,0:T(8,128)(2,1)S(1)} %get-tuple-element.24), channel_id=1, source_target_pairs={{0,13},{1,14},{2,15},{3,0},{4,1},{5,2},{6,3},{7,4},{8,5},{9,6},{10... | collective-permute-start | bytes 221192 | tf_op jit(solution)/shard_map/ppermute | solution.py:377
  60.3 0.9 %join_below.1.refs_3_ = bf16[7,144,2,128]{3,2,1,0:T(2,128)(2,1)} custom-call(f32[4,288,128]{2,1,0:T(8,128)S(1)} %get-tuple-element.25.behind_ref, f32[4,288,128]{2,1,0:T(8,128)S(1)} %get-tuple-element.20.ahead_ref, bf16[288,128]{1,0:T(8,128)(2,1)S(1)} %collective-permute-done.15.refs_0_, bf16[288,128]{1,0:T(8,128)(2,1)S(1)} %collective-permute-done.16.refs_1_, ...), custom_call_target="tpu_custom_call" | custom-call | tf_op jit(solution)/shard_map/join_below/pallas_call | solution.py:338
  61.2 1.8 %collective-permute-done.13.refs_1_ = bf16[288,128]{1,0:T(8,128)(2,1)S(1)} collective-permute-done((bf16[288,128]{1,0:T(8,128)(2,1)S(1)}, bf16[288,128]{1,0:T(8,128)(2,1)S(1)}, u32[]{:S(2)}, u32[]{:S(2)}) %collective-permute-start.13) | collective-permute-done | bytes 73760 | tf_op jit(solution)/shard_map/ppermute | solution.py:377
  63.0 0.6 collective-permute-done.14.refs_2_
  63.6 0.9 %join_above.1 = bf16[7,144,2,128]{3,2,1,0:T(2,128)(2,1)} custom-call(f32[4,288,128]{2,1,0:T(8,128)S(1)} %get-tuple-element.20.ahead_ref, bf16[288,128]{1,0:T(8,128)(2,1)S(1)} %collective-permute-done.12.refs_0_, bf16[288,128]{1,0:T(8,128)(2,1)S(1)} %collective-permute-done.13.refs_1_, ...), custom_call_target="tpu_custom_call", output_to_operand_aliasing={{}: (4, {})} | custom-call | tf_op jit(solution)/shard_map/join_above/pallas_call | solution.py:347
  (14 shorter events, 0.0 us)
Async XLA Ops:
  3.2 21.5 %collective-permute-start.4 = (bf16[12,128,128]{2,1,0:T(8,128)(2,1)S(1)}, bf16[12,128,128]{2,1,0:T(8,128)(2,1)S(1)}, u32[]{:S(2)}, u32[]{:S(2)}) collective-permute-start(bf16[12,128,128]{2,1,0:T(8,128)(2,1)S(1)} %whiten_hour.4.refs_0_), channel_id=1, source_target_pairs={{15,13},{11,9},{7,5},{3,1},{14,12},{10,8},{6,4},{2,0},{13,10},{9,6... | collective-permute-start | bytes 1179656 | tf_op jit(solution)/shard_map/ppermute | solution.py:372
  8.7 24.2 %collective-permute-start.10 = (bf16[12,128,128]{2,1,0:T(8,128)(2,1)S(1)}, bf16[12,128,128]{2,1,0:T(8,128)(2,1)S(1)}, u32[]{:S(2)}, u32[]{:S(2)}) collective-permute-start(bf16[12,128,128]{2,1,0:T(8,128)(2,1)S(1)} %get-tuple-element.21.refs_0_), channel_id=1, source_target_pairs={{0,2},{4,6},{8,10},{12,14},{1,3},{5,7},{9,11},{13,15},{2,5},{6,9},... | collective-permute-start | bytes 1179656 | tf_op jit(solution)/shard_map/ppermute | solution.py:372
  9.3 31.4 %collective-permute-start.1 = (bf16[12,128,128]{2,1,0:T(8,128)(2,1)S(1)}, bf16[12,128,128]{2,1,0:T(8,128)(2,1)S(1)}, u32[]{:S(2)}, u32[]{:S(2)}) collective-permute-start(bf16[12,128,128]{2,1,0:T(8,128)(2,1)S(1)} %whiten_hour.3.refs_0_), channel_id=1, source_target_pairs={{15,13},{11,9},{7,5},{3,1},{14,12},{10,8},{6,4},{2,0},{13,10},{9,6... | collective-permute-start | bytes 1179656 | tf_op jit(solution)/shard_map/ppermute | solution.py:372
  13.8 26.9 %collective-permute-start.3 = (bf16[12,128,128]{2,1,0:T(8,128)(2,1)S(1)}, bf16[12,128,128]{2,1,0:T(8,128)(2,1)S(1)}, u32[]{:S(2)}, u32[]{:S(2)}) collective-permute-start(bf16[12,128,128]{2,1,0:T(8,128)(2,1)S(1)} %whiten_hour.4.refs_0_), channel_id=1, source_target_pairs={{15,14},{11,10},{7,6},{3,2},{13,12},{9,8},{5,4},{1,0},{14,11},{10,... | collective-permute-start | bytes 1179656 | tf_op jit(solution)/shard_map/ppermute | solution.py:372
  24.7 16.5 %collective-permute-start.5 = (bf16[12,128,128]{2,1,0:T(8,128)(2,1)S(1)}, bf16[12,128,128]{2,1,0:T(8,128)(2,1)S(1)}, u32[]{:S(2)}, u32[]{:S(2)}) collective-permute-start(bf16[12,128,128]{2,1,0:T(8,128)(2,1)S(1)} %collective-permute-done.4.refs_2_), channel_id=1, source_target_pairs={{15,14},{11,10},{7,6},{3,2},{14,15},{10,11},{6,7},{2,3},{13,12},{9... | collective-permute-start | bytes 1179656 | tf_op jit(solution)/shard_map/ppermute | solution.py:372
  25.2 19.0 %collective-permute-start.7 = (bf16[12,128,128]{2,1,0:T(8,128)(2,1)S(1)}, bf16[12,128,128]{2,1,0:T(8,128)(2,1)S(1)}, u32[]{:S(2)}, u32[]{:S(2)}) collective-permute-start(bf16[12,128,128]{2,1,0:T(8,128)(2,1)S(1)} %whiten_hour.5.refs_0_), channel_id=1, source_target_pairs={{0,2},{4,6},{8,10},{12,14},{1,3},{5,7},{9,11},{13,15},{2,5},{6,9},... | collective-permute-start | bytes 1179656 | tf_op jit(solution)/shard_map/ppermute | solution.py:372
  32.9 11.3 %collective-permute-start = (bf16[12,128,128]{2,1,0:T(8,128)(2,1)S(1)}, bf16[12,128,128]{2,1,0:T(8,128)(2,1)S(1)}, u32[]{:S(2)}, u32[]{:S(2)}) collective-permute-start(bf16[12,128,128]{2,1,0:T(8,128)(2,1)S(1)} %whiten_hour.3.refs_0_), channel_id=1, source_target_pairs={{15,14},{11,10},{7,6},{3,2},{13,12},{9,8},{5,4},{1,0},{14,11},{10,... | collective-permute-start | bytes 1179656 | tf_op jit(solution)/shard_map/ppermute | solution.py:372
  40.7 5.2 %collective-permute-start.2 = (bf16[12,128,128]{2,1,0:T(8,128)(2,1)S(1)}, bf16[12,128,128]{2,1,0:T(8,128)(2,1)S(1)}, u32[]{:S(2)}, u32[]{:S(2)}) collective-permute-start(bf16[12,128,128]{2,1,0:T(8,128)(2,1)S(1)} %collective-permute-done.1.refs_2_), channel_id=1, source_target_pairs={{15,14},{11,10},{7,6},{3,2},{14,15},{10,11},{6,7},{2,3},{13,12},{9... | collective-permute-start | bytes 1179656 | tf_op jit(solution)/shard_map/ppermute | solution.py:372
  40.7 9.3 %collective-permute-start.9 = (bf16[12,128,128]{2,1,0:T(8,128)(2,1)S(1)}, bf16[12,128,128]{2,1,0:T(8,128)(2,1)S(1)}, u32[]{:S(2)}, u32[]{:S(2)}) collective-permute-start(bf16[12,128,128]{2,1,0:T(8,128)(2,1)S(1)} %get-tuple-element.21.refs_0_), channel_id=1, source_target_pairs={{0,1},{4,5},{8,9},{12,13},{2,3},{6,7},{10,11},{14,15},{1,4},{5,8},... | collective-permute-start | bytes 1179656 | tf_op jit(solution)/shard_map/ppermute | solution.py:372
  41.2 8.8 %collective-permute-start.11 = (bf16[12,128,128]{2,1,0:T(8,128)(2,1)S(1)}, bf16[12,128,128]{2,1,0:T(8,128)(2,1)S(1)}, u32[]{:S(2)}, u32[]{:S(2)}) collective-permute-start(bf16[12,128,128]{2,1,0:T(8,128)(2,1)S(1)} %collective-permute-done.10.refs_2_), channel_id=1, source_target_pairs={{0,1},{4,5},{8,9},{12,13},{1,0},{5,4},{9,8},{13,12},{2,3},{6,7},{1... | collective-permute-start | bytes 1179656 | tf_op jit(solution)/shard_map/ppermute | solution.py:372
  44.1 10.0 %collective-permute-start.6 = (bf16[12,128,128]{2,1,0:T(8,128)(2,1)S(1)}, bf16[12,128,128]{2,1,0:T(8,128)(2,1)S(1)}, u32[]{:S(2)}, u32[]{:S(2)}) collective-permute-start(bf16[12,128,128]{2,1,0:T(8,128)(2,1)S(1)} %whiten_hour.5.refs_0_), channel_id=1, source_target_pairs={{0,1},{4,5},{8,9},{12,13},{2,3},{6,7},{10,11},{14,15},{1,4},{5,8},... | collective-permute-start | bytes 1179656 | tf_op jit(solution)/shard_map/ppermute | solution.py:372
  44.2 9.9 %collective-permute-start.8 = (bf16[12,128,128]{2,1,0:T(8,128)(2,1)S(1)}, bf16[12,128,128]{2,1,0:T(8,128)(2,1)S(1)}, u32[]{:S(2)}, u32[]{:S(2)}) collective-permute-start(bf16[12,128,128]{2,1,0:T(8,128)(2,1)S(1)} %collective-permute-done.7.refs_2_), channel_id=1, source_target_pairs={{0,1},{4,5},{8,9},{12,13},{1,0},{5,4},{9,8},{13,12},{2,3},{6,7},{1... | collective-permute-start | bytes 1179656 | tf_op jit(solution)/shard_map/ppermute | solution.py:372
  48.3 11.3 %collective-permute-start.15 = (bf16[288,128]{1,0:T(8,128)(2,1)S(1)}, bf16[288,128]{1,0:T(8,128)(2,1)S(1)}, u32[]{:S(2)}, u32[]{:S(2)}) collective-permute-start(bf16[288,128]{1,0:T(8,128)(2,1)S(1)} %get-tuple-element.26), channel_id=1, source_target_pairs={{0,1},{1,2},{2,3},{3,4},{4,5},{5,6},{6,7},{7,8},{8,9},{9,10},{10,1... | collective-permute-start | bytes 221192 | tf_op jit(solution)/shard_map/ppermute | solution.py:377
  49.9 10.3 %collective-permute-start.16 = (bf16[288,128]{1,0:T(8,128)(2,1)S(1)}, bf16[288,128]{1,0:T(8,128)(2,1)S(1)}, u32[]{:S(2)}, u32[]{:S(2)}) collective-permute-start(bf16[288,128]{1,0:T(8,128)(2,1)S(1)} %get-tuple-element.27), channel_id=1, source_target_pairs={{0,2},{1,3},{2,4},{3,5},{4,6},{5,7},{6,8},{7,9},{8,10},{9,11},{10,... | collective-permute-start | bytes 221192 | tf_op jit(solution)/shard_map/ppermute | solution.py:377
  50.0 10.3 %collective-permute-start.17 = (bf16[288,128]{1,0:T(8,128)(2,1)S(1)}, bf16[288,128]{1,0:T(8,128)(2,1)S(1)}, u32[]{:S(2)}, u32[]{:S(2)}) collective-permute-start(bf16[288,128]{1,0:T(8,128)(2,1)S(1)} %get-tuple-element.28), channel_id=1, source_target_pairs={{0,3},{1,4},{2,5},{3,6},{4,7},{5,8},{6,9},{7,10},{8,11},{9,12},{10... | collective-permute-start | bytes 221192 | tf_op jit(solution)/shard_map/ppermute | solution.py:377
  56.6 4.6 %collective-permute-start.12 = (bf16[288,128]{1,0:T(8,128)(2,1)S(1)}, bf16[288,128]{1,0:T(8,128)(2,1)S(1)}, u32[]{:S(2)}, u32[]{:S(2)}) collective-permute-start(bf16[288,128]{1,0:T(8,128)(2,1)S(1)} %get-tuple-element.22), channel_id=1, source_target_pairs={{0,15},{1,0},{2,1},{3,2},{4,3},{5,4},{6,5},{7,6},{8,7},{9,8},{10,9... | collective-permute-start | bytes 221192 | tf_op jit(solution)/shard_map/ppermute | solution.py:377
  58.4 4.5 %collective-permute-start.13 = (bf16[288,128]{1,0:T(8,128)(2,1)S(1)}, bf16[288,128]{1,0:T(8,128)(2,1)S(1)}, u32[]{:S(2)}, u32[]{:S(2)}) collective-permute-start(bf16[288,128]{1,0:T(8,128)(2,1)S(1)} %get-tuple-element.23), channel_id=1, source_target_pairs={{0,14},{1,15},{2,0},{3,1},{4,2},{5,3},{6,4},{7,5},{8,6},{9,7},{10,... | collective-permute-start | bytes 221192 | tf_op jit(solution)/shard_map/ppermute | solution.py:377
  59.6 4.0 %collective-permute-start.14 = (bf16[288,128]{1,0:T(8,128)(2,1)S(1)}, bf16[288,128]{1,0:T(8,128)(2,1)S(1)}, u32[]{:S(2)}, u32[]{:S(2)}) collective-permute-start(bf16[288,128]{1,0:T(8,128)(2,1)S(1)} %get-tuple-element.24), channel_id=1, source_target_pairs={{0,13},{1,14},{2,15},{3,0},{4,1},{5,2},{6,3},{7,4},{8,5},{9,6},{10... | collective-permute-start | bytes 221192 | tf_op jit(solution)/shard_map/ppermute | solution.py:377

commit v2 on v1

--- a/solution.py
+++ b/solution.py
@@ -85,39 +85,36 @@
             out_ref[at] = value.astype(jnp.bfloat16)
 
 
+def hour_of(records_hbm, hour, seg_hour):
+    return records_hbm.at[:, pl.ds(hour * seg_hour, seg_hour), :]
+
+
 def whiten_first_kernel(counts_hbm, records_hbm, gap_hbm, table_hbm, *refs):
-    out_ref, rest_ref, valid_ref, table_ref, counts_ref, records_ref, gap_ref, sems = refs
+    out_ref, next_ref, valid_ref, table_ref, counts_ref, records_ref, gap_ref, sems = refs
     seg_hour = records_ref.shape[1]
     hours = valid_ref.shape[0]
-
-    def hour_of(hour):
-        return records_hbm.at[:, pl.ds(hour * seg_hour, seg_hour), :]
-
     moves = [
+        (hour_of(records_hbm, 0, seg_hour), records_ref),
         (counts_hbm, counts_ref),
         (gap_hbm, gap_ref),
         (table_hbm, table_ref),
-        (hour_of(0), records_ref),
+        (hour_of(records_hbm, 1, seg_hour), next_ref),
     ]
-    now = len(moves)
-    moves += [(hour_of(hour), rest_ref.at[hour - 1]) for hour in range(1, hours)]
-    copies = [
+    *copies, ahead = [
         pltpu.make_async_copy(source, target, sems.at[i])
         for i, (source, target) in enumerate(moves)
     ]
-    for copy in copies[:now]:
+    for copy in copies:
         copy.start()
-    for copy in copies[:now]:
+    for copy in copies:
         copy.wait()
-    for copy in copies[now:]:
-        copy.start()
+    ahead.start()
     valid = [validity_rows(hour, seg_hour, counts_ref, gap_ref) for hour in range(hours)]
     for hour in range(1, hours):
         for station, row in enumerate(valid[hour]):
             valid_ref[hour, station : station + 1, :] = row
     whiten_block(records_ref, valid[0], table_ref, out_ref)
-    for copy in copies[now:]:
-        copy.wait()
+    ahead.wait()
 
 
 def whiten_first(records, counts, gap_mask, table):
@@ -131,7 +128,7 @@
         whiten_first_kernel,
         out_shape=[
             jax.ShapeDtypeStruct((channels, samples // 2, LANES), jnp.bfloat16),
-            jax.ShapeDtypeStruct((hours - 1, *block), records.dtype),
+            jax.ShapeDtypeStruct(block, records.dtype),
             jax.ShapeDtypeStruct((hours, stations, LANES), jnp.float32),
             jax.ShapeDtypeStruct(table.shape, table.dtype),
         ],
@@ -141,7 +138,7 @@
             pltpu.SMEM(counts.shape, counts.dtype),
             pltpu.VMEM(block, records.dtype),
             pltpu.VMEM(gap_mask.shape, gap_mask.dtype),
-            pltpu.SemaphoreType.DMA((hours + 3,)),
+            pltpu.SemaphoreType.DMA((5,)),
         ],
         cost_estimate=WHITEN_COST,
         compiler_params=pltpu.CompilerParams(vmem_limit_bytes=4 * MIB),
@@ -154,23 +151,35 @@
     )
 
 
-def whiten_hour_kernel(hour, rest_ref, valid_ref, table_ref, out_ref):
+def whiten_hour_kernel(hour, last, records_hbm, current_ref, valid_ref, table_ref, out_ref, *refs):
+    if not last:
+        next_ref, sem = refs
+        seg_hour = current_ref.shape[1]
+        ahead = pltpu.make_async_copy(hour_of(records_hbm, hour + 1, seg_hour), next_ref, sem)
+        ahead.start()
     valid = [valid_ref[hour, station : station + 1, :] for station in range(valid_ref.shape[1])]
-    whiten_block(rest_ref.at[hour - 1], valid, table_ref, out_ref)
-
-
-def whiten_hour(rest, valid, table, hour):
-    _, channels, _, samples = rest.shape
+    whiten_block(current_ref, valid, table_ref, out_ref)
+    if not last:
+        ahead.wait()
+
+
+def whiten_hour(records, current, valid, table, hour):
+    channels, _, samples = current.shape
+    last = hour + 1 == valid.shape[0]
     vmem = pl.BlockSpec(memory_space=pltpu.VMEM)
+    out_shape = [jax.ShapeDtypeStruct((channels, samples // 2, LANES), jnp.bfloat16)]
+    if not last:
+        out_shape.append(jax.ShapeDtypeStruct(current.shape, current.dtype))
     return pl.pallas_call(
-        lambda *refs: whiten_hour_kernel(hour, *refs),
-        out_shape=jax.ShapeDtypeStruct((channels, samples // 2, LANES), jnp.bfloat16),
-        in_specs=[vmem] * 3,
-        out_specs=vmem,
+        lambda *refs: whiten_hour_kernel(hour, last, *refs),
+        out_shape=out_shape,
+        in_specs=[pl.BlockSpec(memory_space=pltpu.HBM)] + [vmem] * 3,
+        out_specs=[vmem] * len(out_shape),
+        scratch_shapes=[] if last else [pltpu.SemaphoreType.DMA],
         cost_estimate=WHITEN_COST,
         compiler_params=pltpu.CompilerParams(vmem_limit_bytes=4 * MIB),
         name="whiten_hour",
-    )(rest, valid, table)
+    )(pltpu.with_memory_space_constraint(records, pltpu.HBM), current, valid, table)
 
 
 def pair_hour_kernel(hours, first, last, mirrored, *refs):
@@ -409,8 +418,12 @@
     bins = samples // 2
     count = lax.axis_size("sta")
     table = fourier_matrix(samples)
-    first, rest, valid, table = whiten_first(records, counts, gap_mask, table)
-    whitened = [first] + [whiten_hour(rest, valid, table, hour) for hour in range(1, hours)]
+    first, current, valid, table = whiten_first(records, counts, gap_mask, table)
+    whitened = [first]
+    for hour in range(1, hours):
+        block, *ahead = whiten_hour(records, current, valid, table, hour)
+        whitened.append(block)
+        current = ahead[0] if ahead else None
     partners = [fetch_partners(whitened[hour], count, hour) for hour in range(hours)]
     sums = [None, None]
     for hour in range(hours):

time: 64.8 us -> 64.9 us (level)
  waiting for transfers between devices: 30.6 us -> 25.1 us
  starting transfers between devices: 19.8 us -> 24.3 us
  Pallas kernels: 14 us -> 15.2 us
    ppermute x12, waiting for transfers between devices: 28.2 us -> 22.5 us  [send(): return lax.ppermute(value, 'sta', pairs)]
    ppermute x6, starting transfers between devices: 4.88 us -> 7.59 us  [shift(): return lax.ppermute(value, 'sta', pairs)]
    ppermute x12, starting transfers between devices: 14.9 us -> 16.7 us  [send(): return lax.ppermute(value, 'sta', pairs)]
    pallas_call x3, Pallas kernels: 1.53 us -> 3.03 us  [whiten_hour(): pl.pallas_call(lambda *refs: whiten_hour_kernel(hour, last, *refs), out_s...]
  transfers between devices with their start and end apart: 18 -> 18, of which waited for: 7 -> 6; matrix products, arithmetic and copies ran while one was open for 0% -> 0% of each run, Pallas kernels for 15% -> 17%
where the time goes in v2:
time: 64.9 us; the launch traced here: 64.7 us
  waiting for transfers between devices  25.1 us (39%)
  starting transfers between devices  24.3 us (37%)
  Pallas kernels  15.2 us (23%)
    ppermute x12, waiting for transfers between devices, send(): return lax.ppermute(value, 'sta', pairs)  22.5 us
    ppermute x12, starting transfers between devices, send(): return lax.ppermute(value, 'sta', pairs)  16.7 us
    pallas_call x4, Pallas kernels, pair_hour(): pl.pallas_call(lambda *refs: pair_hour_kernel(hours, first, last, mirrore...  7.97 us
    ppermute x6, starting transfers between devices, shift(): return lax.ppermute(value, 'sta', pairs)  7.59 us
    pallas_call x3, Pallas kernels, whiten_hour(): pl.pallas_call(lambda *refs: whiten_hour_kernel(hour, last, *refs), out_s...  3.03 us
    ppermute x6, waiting for transfers between devices, shift(): return lax.ppermute(value, 'sta', pairs)  2.63 us
    pallas_call x1, Pallas kernels, whiten_first(): pl.pallas_call(whiten_first_kernel, out_shape=[jax.ShapeDtypeStruct((chan...  2.36 us
  transfers between devices with their start and end apart: 18, of which 6 were waited for; matrix products, arithmetic and copies ran while one was open for 0% of the time, Pallas kernels for 17%

profile of v2, /device:TPU:0, one launch (start us, length us, event | category | flops | bytes accessed | tf_op | source)
XLA Modules:
  0.0 64.7 jit_solution(4148796018617981354)
XLA Ops:
  0.0 2.4 %whiten_first.1 = (bf16[12,128,128]{2,1,0:T(8,128)(2,1)S(1)}, bf16[12,64,256]{2,1,0:T(8,128)(2,1)S(1)}, f32[4,4,128]{2,1,0:T(4,128)S(1)}, bf16[256,256]{1,0:T(8,128)(2,1)S(1)}) custom-call(s32[4,4]{1,0:T(4,128)} %counts_hbm.1, bf16[12,256,256]{2,1,0:T(8,128)(2,1)} %refs_0_.5, s32[4,256]{1,0:T(4,128)} %gap_hbm.1, bf16[256,256]{1,0:T(8,128)(2,1)} %constant.2.clone.table_hbm), custom_call_target="tpu_custom_call" | custom-call | flops 2000000000 | bytes 8000000 | tf_op jit(solution)/shard_map/whiten_first/pallas_call | solution.py:127
  2.4 1.3 %whiten_hour.3 = (bf16[12,128,128]{2,1,0:T(8,128)(2,1)S(1)}, bf16[12,64,256]{2,1,0:T(8,128)(2,1)S(1)}) custom-call(bf16[12,256,256]{2,1,0:T(8,128)(2,1)} %refs_0_.5, bf16[12,64,256]{2,1,0:T(8,128)(2,1)S(1)} %get-tuple-element.21.refs_1_, f32[4,4,128]{2,1,0:T(4,128)S(1)} %get-tuple-element.22.refs_2_, bf16[256,256]{1,0:T(8,128)(2,1)S(1)} %get-tuple-element.23.refs_3_), custom_call_target="tpu_custom_call" | custom-call | flops 2000000000 | bytes 8000000 | tf_op jit(solution)/shard_map/whiten_hour/pallas_call | solution.py:173
  3.6 5.5 %collective-permute-start.4 = (bf16[12,128,128]{2,1,0:T(8,128)(2,1)S(1)}, bf16[12,128,128]{2,1,0:T(8,128)(2,1)S(1)}, u32[]{:S(2)}, u32[]{:S(2)}) collective-permute-start(bf16[12,128,128]{2,1,0:T(8,128)(2,1)S(1)} %get-tuple-element.26.refs_0_), channel_id=1, source_target_pairs={{15,13},{11,9},{7,5},{3,1},{14,12},{10,8},{6,4},{2,0},{13,10},{9,6... | collective-permute-start | bytes 1179656 | tf_op jit(solution)/shard_map/ppermute | solution.py:381
  9.2 1.3 %whiten_hour.4 = (bf16[12,128,128]{2,1,0:T(8,128)(2,1)S(1)}, bf16[12,64,256]{2,1,0:T(8,128)(2,1)S(1)}) custom-call(bf16[12,256,256]{2,1,0:T(8,128)(2,1)} %refs_0_.5, bf16[12,64,256]{2,1,0:T(8,128)(2,1)S(1)} %get-tuple-element.24.refs_1_, f32[4,4,128]{2,1,0:T(4,128)S(1)} %get-tuple-element.22.refs_2_, bf16[256,256]{1,0:T(8,128)(2,1)S(1)} %get-tuple-element.23.refs_3_), custom_call_target="tpu_custom_call" | custom-call | flops 2000000000 | bytes 8000000 | tf_op jit(solution)/shard_map/whiten_hour/pallas_call | solution.py:173
  10.4 0.5 whiten_hour.5.refs_0_
  11.0 0.3 collective-permute-start.1
  11.2 1.0 %collective-permute-start.3 = (bf16[12,128,128]{2,1,0:T(8,128)(2,1)S(1)}, bf16[12,128,128]{2,1,0:T(8,128)(2,1)S(1)}, u32[]{:S(2)}, u32[]{:S(2)}) collective-permute-start(bf16[12,128,128]{2,1,0:T(8,128)(2,1)S(1)} %get-tuple-element.26.refs_0_), channel_id=1, source_target_pairs={{15,14},{11,10},{7,6},{3,2},{13,12},{9,8},{5,4},{1,0},{14,11},{10,... | collective-permute-start | bytes 1179656 | tf_op jit(solution)/shard_map/ppermute | solution.py:381
  12.3 1.2 %collective-permute-start.10 = (bf16[12,128,128]{2,1,0:T(8,128)(2,1)S(1)}, bf16[12,128,128]{2,1,0:T(8,128)(2,1)S(1)}, u32[]{:S(2)}, u32[]{:S(2)}) collective-permute-start(bf16[12,128,128]{2,1,0:T(8,128)(2,1)S(1)} %get-tuple-element.29.refs_0_), channel_id=1, source_target_pairs={{0,2},{4,6},{8,10},{12,14},{1,3},{5,7},{9,11},{13,15},{2,5},{6,9},... | collective-permute-start | bytes 1179656 | tf_op jit(solution)/shard_map/ppermute | solution.py:381
  13.5 5.2 %collective-permute-done.4.refs_2_ = bf16[12,128,128]{2,1,0:T(8,128)(2,1)S(1)} collective-permute-done((bf16[12,128,128]{2,1,0:T(8,128)(2,1)S(1)}, bf16[12,128,128]{2,1,0:T(8,128)(2,1)S(1)}, u32[]{:S(2)}, u32[]{:S(2)}) %collective-permute-start.4) | collective-permute-done | bytes 393248 | tf_op jit(solution)/shard_map/ppermute | solution.py:381
  18.7 0.1 collective-permute-start.5
  18.8 6.8 %collective-permute-start = (bf16[12,128,128]{2,1,0:T(8,128)(2,1)S(1)}, bf16[12,128,128]{2,1,0:T(8,128)(2,1)S(1)}, u32[]{:S(2)}, u32[]{:S(2)}) collective-permute-start(bf16[12,128,128]{2,1,0:T(8,128)(2,1)S(1)} %whiten_hour.5.refs_0_), channel_id=1, source_target_pairs={{15,14},{11,10},{7,6},{3,2},{13,12},{9,8},{5,4},{1,0},{14,11},{10,... | collective-permute-start | bytes 1179656 | tf_op jit(solution)/shard_map/ppermute | solution.py:381
  25.5 7.1 %collective-permute-done.1.refs_2_ = bf16[12,128,128]{2,1,0:T(8,128)(2,1)S(1)} collective-permute-done((bf16[12,128,128]{2,1,0:T(8,128)(2,1)S(1)}, bf16[12,128,128]{2,1,0:T(8,128)(2,1)S(1)}, u32[]{:S(2)}, u32[]{:S(2)}) %collective-permute-start.1) | collective-permute-done | bytes 393248 | tf_op jit(solution)/shard_map/ppermute | solution.py:381
  32.7 0.0 collective-permute-start.7
  32.7 0.0 collective-permute-done.3.refs_1_
  32.7 0.8 %collective-permute-done.10.refs_2_ = bf16[12,128,128]{2,1,0:T(8,128)(2,1)S(1)} collective-permute-done((bf16[12,128,128]{2,1,0:T(8,128)(2,1)S(1)}, bf16[12,128,128]{2,1,0:T(8,128)(2,1)S(1)}, u32[]{:S(2)}, u32[]{:S(2)}) %collective-permute-start.10) | collective-permute-done | bytes 393248 | tf_op jit(solution)/shard_map/ppermute | solution.py:381
  33.5 1.7 %collective-permute-start.11 = (bf16[12,128,128]{2,1,0:T(8,128)(2,1)S(1)}, bf16[12,128,128]{2,1,0:T(8,128)(2,1)S(1)}, u32[]{:S(2)}, u32[]{:S(2)}) collective-permute-start(bf16[12,128,128]{2,1,0:T(8,128)(2,1)S(1)} %collective-permute-done.10.refs_2_), channel_id=1, source_target_pairs={{0,1},{4,5},{8,9},{12,13},{1,0},{5,4},{9,8},{13,12},{2,3},{6,7},{1... | collective-permute-start | bytes 1179656 | tf_op jit(solution)/shard_map/ppermute | solution.py:381
  35.2 1.6 %pair_hour.2.refs_4_ = f32[2048,128]{1,0:T(8,128)S(1)} custom-call(bf16[12,128,128]{2,1,0:T(8,128)(2,1)S(1)} %get-tuple-element.26.refs_0_, bf16[12,128,128]{2,1,0:T(8,128)(2,1)S(1)} %collective-permute-done.3.refs_1_, bf16[12,128,128]{2,1,0:T(8,128)(2,1)S(1)} %collective-permute-done.4.refs_2_, bf16[12,128,128]{2,1,0:T(8,128)(2,1)S(1)} %collective-permute-done.5.refs_3_), custom_call_target="tpu_custom_call" | custom-call | flops 3000000000 | bytes 12000000 | tf_op jit(solution)/shard_map/pair_hour/pallas_call | solution.py:312
  36.7 0.1 collective-permute-start.6
  36.8 9.4 %collective-permute-done.7.refs_2_ = bf16[12,128,128]{2,1,0:T(8,128)(2,1)S(1)} collective-permute-done((bf16[12,128,128]{2,1,0:T(8,128)(2,1)S(1)}, bf16[12,128,128]{2,1,0:T(8,128)(2,1)S(1)}, u32[]{:S(2)}, u32[]{:S(2)}) %collective-permute-start.7) | collective-permute-done | bytes 393248 | tf_op jit(solution)/shard_map/ppermute | solution.py:381
  46.2 2.4 %pair_hour_last.2 = (f32[4,288,128]{2,1,0:T(8,128)S(1)}, bf16[288,128]{1,0:T(8,128)(2,1)S(1)}, bf16[288,128]{1,0:T(8,128)(2,1)S(1)}, bf16[288,128]{1,0:T(8,128)(2,1)S(1)}) custom-call(bf16[12,128,128]{2,1,0:T(8,128)(2,1)S(1)} %whiten_hour.5.refs_0_, bf16[12,128,128]{2,1,0:T(8,128)(2,1)S(1)} %collective-permute-done.refs_1_, ...), custom_call_target="tpu_custom_call" | custom-call | flops 3000000000 | bytes 12000000 | tf_op jit(solution)/shard_map/pair_hour_last/pallas_call | solution.py:312
  48.7 0.6 collective-permute-start.15
  49.2 1.8 %collective-permute-start.16 = (bf16[288,128]{1,0:T(8,128)(2,1)S(1)}, bf16[288,128]{1,0:T(8,128)(2,1)S(1)}, u32[]{:S(2)}, u32[]{:S(2)}) collective-permute-start(bf16[288,128]{1,0:T(8,128)(2,1)S(1)} %get-tuple-element.35), channel_id=1, source_target_pairs={{0,2},{1,3},{2,4},{3,5},{4,6},{5,7},{6,8},{7,9},{8,10},{9,11},{10,... | collective-permute-start | bytes 221192 | tf_op jit(solution)/shard_map/ppermute | solution.py:386
  51.0 1.6 %pair_hour.3.refs_4_ = f32[2048,128]{1,0:T(8,128)S(1)} custom-call(bf16[12,128,128]{2,1,0:T(8,128)(2,1)S(1)} %get-tuple-element.29.refs_0_, bf16[12,128,128]{2,1,0:T(8,128)(2,1)S(1)} %collective-permute-done.9.refs_1_, bf16[12,128,128]{2,1,0:T(8,128)(2,1)S(1)} %collective-permute-done.10.refs_2_, bf16[12,128,128]{2,1,0:T(8,128)(2,1)S(1)} %collective-permute-done.11.refs_3_), custom_call_target="tpu_custom_call" | custom-call | flops 3000000000 | bytes 12000000 | tf_op jit(solution)/shard_map/pair_hour/pallas_call | solution.py:312
  52.5 0.0 collective-permute-done.8.refs_3_
  52.6 2.4 %pair_hour_last.3 = (f32[4,288,128]{2,1,0:T(8,128)S(1)}, bf16[288,128]{1,0:T(8,128)(2,1)S(1)}, bf16[288,128]{1,0:T(8,128)(2,1)S(1)}, bf16[288,128]{1,0:T(8,128)(2,1)S(1)}) custom-call(bf16[12,128,128]{2,1,0:T(8,128)(2,1)S(1)} %get-tuple-element.28.refs_0_, bf16[12,128,128]{2,1,0:T(8,128)(2,1)S(1)} %collective-permute-done.6.refs_1_, ...), custom_call_target="tpu_custom_call" | custom-call | flops 3000000000 | bytes 12000000 | tf_op jit(solution)/shard_map/pair_hour_last/pallas_call | solution.py:312
  55.0 3.0 %collective-permute-start.12 = (bf16[288,128]{1,0:T(8,128)(2,1)S(1)}, bf16[288,128]{1,0:T(8,128)(2,1)S(1)}, u32[]{:S(2)}, u32[]{:S(2)}) collective-permute-start(bf16[288,128]{1,0:T(8,128)(2,1)S(1)} %get-tuple-element.30), channel_id=1, source_target_pairs={{0,15},{1,0},{2,1},{3,2},{4,3},{5,4},{6,5},{7,6},{8,7},{9,8},{10,9... | collective-permute-start | bytes 221192 | tf_op jit(solution)/shard_map/ppermute | solution.py:386
  58.0 2.0 %collective-permute-start.13 = (bf16[288,128]{1,0:T(8,128)(2,1)S(1)}, bf16[288,128]{1,0:T(8,128)(2,1)S(1)}, u32[]{:S(2)}, u32[]{:S(2)}) collective-permute-start(bf16[288,128]{1,0:T(8,128)(2,1)S(1)} %get-tuple-element.31), channel_id=1, source_target_pairs={{0,14},{1,15},{2,0},{3,1},{4,2},{5,3},{6,4},{7,5},{8,6},{9,7},{10,... | collective-permute-start | bytes 221192 | tf_op jit(solution)/shard_map/ppermute | solution.py:386
  60.1 0.2 collective-permute-start.14
  60.3 0.9 %join_below.1.refs_3_ = bf16[7,144,2,128]{3,2,1,0:T(2,128)(2,1)} custom-call(f32[4,288,128]{2,1,0:T(8,128)S(1)} %get-tuple-element.33.behind_ref, f32[4,288,128]{2,1,0:T(8,128)S(1)} %get-tuple-element.27.ahead_ref, bf16[288,128]{1,0:T(8,128)(2,1)S(1)} %collective-permute-done.15.refs_0_, bf16[288,128]{1,0:T(8,128)(2,1)S(1)} %collective-permute-done.16.refs_1_, ...), custom_call_target="tpu_custom_call" | custom-call | tf_op jit(solution)/shard_map/join_below/pallas_call | solution.py:347
  61.2 1.2 %collective-permute-done.13.refs_1_ = bf16[288,128]{1,0:T(8,128)(2,1)S(1)} collective-permute-done((bf16[288,128]{1,0:T(8,128)(2,1)S(1)}, bf16[288,128]{1,0:T(8,128)(2,1)S(1)}, u32[]{:S(2)}, u32[]{:S(2)}) %collective-permute-start.13) | collective-permute-done | bytes 73760 | tf_op jit(solution)/shard_map/ppermute | solution.py:386
  62.4 1.4 %collective-permute-done.14.refs_2_ = bf16[288,128]{1,0:T(8,128)(2,1)S(1)} collective-permute-done((bf16[288,128]{1,0:T(8,128)(2,1)S(1)}, bf16[288,128]{1,0:T(8,128)(2,1)S(1)}, u32[]{:S(2)}, u32[]{:S(2)}) %collective-permute-start.14) | collective-permute-done | bytes 73760 | tf_op jit(solution)/shard_map/ppermute | solution.py:386
  63.8 0.9 %join_above.1 = bf16[7,144,2,128]{3,2,1,0:T(2,128)(2,1)} custom-call(f32[4,288,128]{2,1,0:T(8,128)S(1)} %get-tuple-element.27.ahead_ref, bf16[288,128]{1,0:T(8,128)(2,1)S(1)} %collective-permute-done.12.refs_0_, bf16[288,128]{1,0:T(8,128)(2,1)S(1)} %collective-permute-done.13.refs_1_, ...), custom_call_target="tpu_custom_call", output_to_operand_aliasing={{}: (4, {})} | custom-call | tf_op jit(solution)/shard_map/join_above/pallas_call | solution.py:356
  (14 shorter events, 0.0 us)
Async XLA Ops:
  3.6 15.0 %collective-permute-start.4 = (bf16[12,128,128]{2,1,0:T(8,128)(2,1)S(1)}, bf16[12,128,128]{2,1,0:T(8,128)(2,1)S(1)}, u32[]{:S(2)}, u32[]{:S(2)}) collective-permute-start(bf16[12,128,128]{2,1,0:T(8,128)(2,1)S(1)} %get-tuple-element.26.refs_0_), channel_id=1, source_target_pairs={{15,13},{11,9},{7,5},{3,1},{14,12},{10,8},{6,4},{2,0},{13,10},{9,6... | collective-permute-start | bytes 1179656 | tf_op jit(solution)/shard_map/ppermute | solution.py:381
  11.0 21.7 %collective-permute-start.1 = (bf16[12,128,128]{2,1,0:T(8,128)(2,1)S(1)}, bf16[12,128,128]{2,1,0:T(8,128)(2,1)S(1)}, u32[]{:S(2)}, u32[]{:S(2)}) collective-permute-start(bf16[12,128,128]{2,1,0:T(8,128)(2,1)S(1)} %whiten_hour.5.refs_0_), channel_id=1, source_target_pairs={{15,13},{11,9},{7,5},{3,1},{14,12},{10,8},{6,4},{2,0},{13,10},{9,6... | collective-permute-start | bytes 1179656 | tf_op jit(solution)/shard_map/ppermute | solution.py:381
  11.2 21.4 %collective-permute-start.3 = (bf16[12,128,128]{2,1,0:T(8,128)(2,1)S(1)}, bf16[12,128,128]{2,1,0:T(8,128)(2,1)S(1)}, u32[]{:S(2)}, u32[]{:S(2)}) collective-permute-start(bf16[12,128,128]{2,1,0:T(8,128)(2,1)S(1)} %get-tuple-element.26.refs_0_), channel_id=1, source_target_pairs={{15,14},{11,10},{7,6},{3,2},{13,12},{9,8},{5,4},{1,0},{14,11},{10,... | collective-permute-start | bytes 1179656 | tf_op jit(solution)/shard_map/ppermute | solution.py:381
  12.3 21.2 %collective-permute-start.10 = (bf16[12,128,128]{2,1,0:T(8,128)(2,1)S(1)}, bf16[12,128,128]{2,1,0:T(8,128)(2,1)S(1)}, u32[]{:S(2)}, u32[]{:S(2)}) collective-permute-start(bf16[12,128,128]{2,1,0:T(8,128)(2,1)S(1)} %get-tuple-element.29.refs_0_), channel_id=1, source_target_pairs={{0,2},{4,6},{8,10},{12,14},{1,3},{5,7},{9,11},{13,15},{2,5},{6,9},... | collective-permute-start | bytes 1179656 | tf_op jit(solution)/shard_map/ppermute | solution.py:381
  18.7 14.8 %collective-permute-start.5 = (bf16[12,128,128]{2,1,0:T(8,128)(2,1)S(1)}, bf16[12,128,128]{2,1,0:T(8,128)(2,1)S(1)}, u32[]{:S(2)}, u32[]{:S(2)}) collective-permute-start(bf16[12,128,128]{2,1,0:T(8,128)(2,1)S(1)} %collective-permute-done.4.refs_2_), channel_id=1, source_target_pairs={{15,14},{11,10},{7,6},{3,2},{14,15},{10,11},{6,7},{2,3},{13,12},{9... | collective-permute-start | bytes 1179656 | tf_op jit(solution)/shard_map/ppermute | solution.py:381
  18.8 18.0 %collective-permute-start = (bf16[12,128,128]{2,1,0:T(8,128)(2,1)S(1)}, bf16[12,128,128]{2,1,0:T(8,128)(2,1)S(1)}, u32[]{:S(2)}, u32[]{:S(2)}) collective-permute-start(bf16[12,128,128]{2,1,0:T(8,128)(2,1)S(1)} %whiten_hour.5.refs_0_), channel_id=1, source_target_pairs={{15,14},{11,10},{7,6},{3,2},{13,12},{9,8},{5,4},{1,0},{14,11},{10,... | collective-permute-start | bytes 1179656 | tf_op jit(solution)/shard_map/ppermute | solution.py:381
  32.7 13.5 %collective-permute-start.7 = (bf16[12,128,128]{2,1,0:T(8,128)(2,1)S(1)}, bf16[12,128,128]{2,1,0:T(8,128)(2,1)S(1)}, u32[]{:S(2)}, u32[]{:S(2)}) collective-permute-start(bf16[12,128,128]{2,1,0:T(8,128)(2,1)S(1)} %get-tuple-element.28.refs_0_), channel_id=1, source_target_pairs={{0,2},{4,6},{8,10},{12,14},{1,3},{5,7},{9,11},{13,15},{2,5},{6,9},... | collective-permute-start | bytes 1179656 | tf_op jit(solution)/shard_map/ppermute | solution.py:381
  32.7 13.5 %collective-permute-start.2 = (bf16[12,128,128]{2,1,0:T(8,128)(2,1)S(1)}, bf16[12,128,128]{2,1,0:T(8,128)(2,1)S(1)}, u32[]{:S(2)}, u32[]{:S(2)}) collective-permute-start(bf16[12,128,128]{2,1,0:T(8,128)(2,1)S(1)} %collective-permute-done.1.refs_2_), channel_id=1, source_target_pairs={{15,14},{11,10},{7,6},{3,2},{14,15},{10,11},{6,7},{2,3},{13,12},{9... | collective-permute-start | bytes 1179656 | tf_op jit(solution)/shard_map/ppermute | solution.py:381
  33.5 15.8 %collective-permute-start.9 = (bf16[12,128,128]{2,1,0:T(8,128)(2,1)S(1)}, bf16[12,128,128]{2,1,0:T(8,128)(2,1)S(1)}, u32[]{:S(2)}, u32[]{:S(2)}) collective-permute-start(bf16[12,128,128]{2,1,0:T(8,128)(2,1)S(1)} %get-tuple-element.29.refs_0_), channel_id=1, source_target_pairs={{0,1},{4,5},{8,9},{12,13},{2,3},{6,7},{10,11},{14,15},{1,4},{5,8},... | collective-permute-start | bytes 1179656 | tf_op jit(solution)/shard_map/ppermute | solution.py:381
  33.5 17.5 %collective-permute-start.11 = (bf16[12,128,128]{2,1,0:T(8,128)(2,1)S(1)}, bf16[12,128,128]{2,1,0:T(8,128)(2,1)S(1)}, u32[]{:S(2)}, u32[]{:S(2)}) collective-permute-start(bf16[12,128,128]{2,1,0:T(8,128)(2,1)S(1)} %collective-permute-done.10.refs_2_), channel_id=1, source_target_pairs={{0,1},{4,5},{8,9},{12,13},{1,0},{5,4},{9,8},{13,12},{2,3},{6,7},{1... | collective-permute-start | bytes 1179656 | tf_op jit(solution)/shard_map/ppermute | solution.py:381
  36.7 15.8 %collective-permute-start.6 = (bf16[12,128,128]{2,1,0:T(8,128)(2,1)S(1)}, bf16[12,128,128]{2,1,0:T(8,128)(2,1)S(1)}, u32[]{:S(2)}, u32[]{:S(2)}) collective-permute-start(bf16[12,128,128]{2,1,0:T(8,128)(2,1)S(1)} %get-tuple-element.28.refs_0_), channel_id=1, source_target_pairs={{0,1},{4,5},{8,9},{12,13},{2,3},{6,7},{10,11},{14,15},{1,4},{5,8},... | collective-permute-start | bytes 1179656 | tf_op jit(solution)/shard_map/ppermute | solution.py:381
  46.2 6.4 %collective-permute-start.8 = (bf16[12,128,128]{2,1,0:T(8,128)(2,1)S(1)}, bf16[12,128,128]{2,1,0:T(8,128)(2,1)S(1)}, u32[]{:S(2)}, u32[]{:S(2)}) collective-permute-start(bf16[12,128,128]{2,1,0:T(8,128)(2,1)S(1)} %collective-permute-done.7.refs_2_), channel_id=1, source_target_pairs={{0,1},{4,5},{8,9},{12,13},{1,0},{5,4},{9,8},{13,12},{2,3},{6,7},{1... | collective-permute-start | bytes 1179656 | tf_op jit(solution)/shard_map/ppermute | solution.py:381
  48.7 11.4 %collective-permute-start.15 = (bf16[288,128]{1,0:T(8,128)(2,1)S(1)}, bf16[288,128]{1,0:T(8,128)(2,1)S(1)}, u32[]{:S(2)}, u32[]{:S(2)}) collective-permute-start(bf16[288,128]{1,0:T(8,128)(2,1)S(1)} %get-tuple-element.34), channel_id=1, source_target_pairs={{0,1},{1,2},{2,3},{3,4},{4,5},{5,6},{6,7},{7,8},{8,9},{9,10},{10,1... | collective-permute-start | bytes 221192 | tf_op jit(solution)/shard_map/ppermute | solution.py:386
  49.2 11.0 %collective-permute-start.16 = (bf16[288,128]{1,0:T(8,128)(2,1)S(1)}, bf16[288,128]{1,0:T(8,128)(2,1)S(1)}, u32[]{:S(2)}, u32[]{:S(2)}) collective-permute-start(bf16[288,128]{1,0:T(8,128)(2,1)S(1)} %get-tuple-element.35), channel_id=1, source_target_pairs={{0,2},{1,3},{2,4},{3,5},{4,6},{5,7},{6,8},{7,9},{8,10},{9,11},{10,... | collective-permute-start | bytes 221192 | tf_op jit(solution)/shard_map/ppermute | solution.py:386
  51.0 9.3 %collective-permute-start.17 = (bf16[288,128]{1,0:T(8,128)(2,1)S(1)}, bf16[288,128]{1,0:T(8,128)(2,1)S(1)}, u32[]{:S(2)}, u32[]{:S(2)}) collective-permute-start(bf16[288,128]{1,0:T(8,128)(2,1)S(1)} %get-tuple-element.36), channel_id=1, source_target_pairs={{0,3},{1,4},{2,5},{3,6},{4,7},{5,8},{6,9},{7,10},{8,11},{9,12},{10... | collective-permute-start | bytes 221192 | tf_op jit(solution)/shard_map/ppermute | solution.py:386
  55.0 6.2 %collective-permute-start.12 = (bf16[288,128]{1,0:T(8,128)(2,1)S(1)}, bf16[288,128]{1,0:T(8,128)(2,1)S(1)}, u32[]{:S(2)}, u32[]{:S(2)}) collective-permute-start(bf16[288,128]{1,0:T(8,128)(2,1)S(1)} %get-tuple-element.30), channel_id=1, source_target_pairs={{0,15},{1,0},{2,1},{3,2},{4,3},{5,4},{6,5},{7,6},{8,7},{9,8},{10,9... | collective-permute-start | bytes 221192 | tf_op jit(solution)/shard_map/ppermute | solution.py:386
  58.0 4.4 %collective-permute-start.13 = (bf16[288,128]{1,0:T(8,128)(2,1)S(1)}, bf16[288,128]{1,0:T(8,128)(2,1)S(1)}, u32[]{:S(2)}, u32[]{:S(2)}) collective-permute-start(bf16[288,128]{1,0:T(8,128)(2,1)S(1)} %get-tuple-element.31), channel_id=1, source_target_pairs={{0,14},{1,15},{2,0},{3,1},{4,2},{5,3},{6,4},{7,5},{8,6},{9,7},{10,... | collective-permute-start | bytes 221192 | tf_op jit(solution)/shard_map/ppermute | solution.py:386
  60.1 3.8 %collective-permute-start.14 = (bf16[288,128]{1,0:T(8,128)(2,1)S(1)}, bf16[288,128]{1,0:T(8,128)(2,1)S(1)}, u32[]{:S(2)}, u32[]{:S(2)}) collective-permute-start(bf16[288,128]{1,0:T(8,128)(2,1)S(1)} %get-tuple-element.32), channel_id=1, source_target_pairs={{0,13},{1,14},{2,15},{3,0},{4,1},{5,2},{6,3},{7,4},{8,5},{9,6},{10... | collective-permute-start | bytes 221192 | tf_op jit(solution)/shard_map/ppermute | solution.py:386

commit v3 on v1

--- a/solution.py
+++ b/solution.py
@@ -10,11 +10,13 @@
 
 
 ROUNDS = 3
+COMPONENTS = 3
 LANES = 128
 PITCH = 16
 SKEW = 8
 MIB = 1 << 20
 PAIR_LIMIT = 10 * MIB
+FETCHES = COMPONENTS
 PAIR_COST = pl.CostEstimate(flops=3_000_000_000, transcendentals=0, bytes_accessed=12_000_000)
 WHITEN_COST = pl.CostEstimate(flops=2_000_000_000, transcendentals=0, bytes_accessed=8_000_000)
 
@@ -90,27 +92,30 @@
     seg_hour = records_ref.shape[1]
     hours = valid_ref.shape[0]
 
-    def hour_of(hour):
-        return records_hbm.at[:, pl.ds(hour * seg_hour, seg_hour), :]
-
-    moves = [
-        (counts_hbm, counts_ref),
-        (gap_hbm, gap_ref),
-        (table_hbm, table_ref),
-        (hour_of(0), records_ref),
-    ]
+    channels = records_ref.shape[0]
+
+    def parts(hour, target, count):
+        size = channels // count
+        for part in range(count):
+            span = pl.ds(part * size, size)
+            yield (
+                records_hbm.at[span, pl.ds(hour * seg_hour, seg_hour), :],
+                target.at[span],
+            )
+
+    moves = list(parts(0, records_ref, channels))
+    moves += [(counts_hbm, counts_ref), (gap_hbm, gap_ref), (table_hbm, table_ref)]
     now = len(moves)
-    moves += [(hour_of(hour), rest_ref.at[hour - 1]) for hour in range(1, hours)]
+    for hour in range(1, hours):
+        moves += parts(hour, rest_ref.at[hour - 1], FETCHES)
     copies = [
         pltpu.make_async_copy(source, target, sems.at[i])
         for i, (source, target) in enumerate(moves)
     ]
-    for copy in copies[:now]:
+    for copy in copies:
         copy.start()
     for copy in copies[:now]:
         copy.wait()
-    for copy in copies[now:]:
-        copy.start()
     valid = [validity_rows(hour, seg_hour, counts_ref, gap_ref) for hour in range(hours)]
     for hour in range(1, hours):
         for station, row in enumerate(valid[hour]):
@@ -141,7 +146,7 @@
             pltpu.SMEM(counts.shape, counts.dtype),
             pltpu.VMEM(block, records.dtype),
             pltpu.VMEM(gap_mask.shape, gap_mask.dtype),
-            pltpu.SemaphoreType.DMA((hours + 3,)),
+            pltpu.SemaphoreType.DMA((channels + 3 + (hours - 1) * FETCHES,)),
         ],
         cost_estimate=WHITEN_COST,
         compiler_params=pltpu.CompilerParams(vmem_limit_bytes=4 * MIB),

time: 64.8 us -> 64 us (0.988)
  Pallas kernels: 14 us -> 13.2 us
    pallas_call x1, Pallas kernels: 2.68 us -> 1.86 us  [whiten_first(): pl.pallas_call(whiten_first_kernel, out_shape=[jax.ShapeDtypeStruct((chan...]
  transfers between devices with their start and end apart: 18 -> 18, of which waited for: 7 -> 7; matrix products, arithmetic and copies ran while one was open for 0% -> 0% of each run, Pallas kernels for 15% -> 16%
where the time goes in v3:
time: 64 us; the launch traced here: 63.6 us
  waiting for transfers between devices  30.6 us (48%)
  starting transfers between devices  19.7 us (31%)
  Pallas kernels  13.2 us (21%)
    ppermute x12, waiting for transfers between devices, send(): return lax.ppermute(value, 'sta', pairs)  28.2 us
    ppermute x12, starting transfers between devices, send(): return lax.ppermute(value, 'sta', pairs)  14.9 us
    pallas_call x4, Pallas kernels, pair_hour(): pl.pallas_call(lambda *refs: pair_hour_kernel(hours, first, last, mirrore...  7.97 us
    ppermute x6, starting transfers between devices, shift(): return lax.ppermute(value, 'sta', pairs)  4.88 us
    ppermute x6, waiting for transfers between devices, shift(): return lax.ppermute(value, 'sta', pairs)  2.37 us
    pallas_call x1, Pallas kernels, whiten_first(): pl.pallas_call(whiten_first_kernel, out_shape=[jax.ShapeDtypeStruct((chan...  1.86 us
    pallas_call x3, Pallas kernels, whiten_hour(): pl.pallas_call(lambda *refs: whiten_hour_kernel(hour, *refs), out_shape=j...  1.53 us
  transfers between devices with their start and end apart: 18, of which 7 were waited for; matrix products, arithmetic and copies ran while one was open for 0% of the time, Pallas kernels for 16%

profile of v3, /device:TPU:0, one launch (start us, length us, event | category | flops | bytes accessed | tf_op | source)
XLA Modules:
  0.0 63.6 jit_solution(6440218905917231769)
XLA Ops:
  0.0 1.9 %whiten_first.1 = (bf16[12,128,128]{2,1,0:T(8,128)(2,1)S(1)}, bf16[3,12,64,256]{3,2,1,0:T(8,128)(2,1)S(1)}, f32[4,4,128]{2,1,0:T(4,128)S(1)}, bf16[256,256]{1,0:T(8,128)(2,1)S(1)}) custom-call(s32[4,4]{1,0:T(4,128)} %counts_hbm.1, bf16[12,256,256]{2,1,0:T(8,128)(2,1)} %records_hbm.1, s32[4,256]{1,0:T(4,128)} %gap_hbm.1, bf16[256,256]{1,0:T(8,128)(2,1)} %constant.2.clone.table_hbm), custom_call_target="tpu_custom_call" | custom-call | flops 2000000000 | bytes 8000000 | tf_op jit(solution)/shard_map/whiten_first/pallas_call | solution.py:135
  1.9 0.5 whiten_hour.4.refs_0_
  2.4 5.5 %collective-permute-start.4 = (bf16[12,128,128]{2,1,0:T(8,128)(2,1)S(1)}, bf16[12,128,128]{2,1,0:T(8,128)(2,1)S(1)}, u32[]{:S(2)}, u32[]{:S(2)}) collective-permute-start(bf16[12,128,128]{2,1,0:T(8,128)(2,1)S(1)} %whiten_hour.4.refs_0_), channel_id=1, source_target_pairs={{15,13},{11,9},{7,5},{3,1},{14,12},{10,8},{6,4},{2,0},{13,10},{9,6... | collective-permute-start | bytes 1179656 | tf_op jit(solution)/shard_map/ppermute | solution.py:377
  7.9 0.5 whiten_hour.3.refs_0_
  8.4 4.5 %collective-permute-start.1 = (bf16[12,128,128]{2,1,0:T(8,128)(2,1)S(1)}, bf16[12,128,128]{2,1,0:T(8,128)(2,1)S(1)}, u32[]{:S(2)}, u32[]{:S(2)}) collective-permute-start(bf16[12,128,128]{2,1,0:T(8,128)(2,1)S(1)} %whiten_hour.3.refs_0_), channel_id=1, source_target_pairs={{15,13},{11,9},{7,5},{3,1},{14,12},{10,8},{6,4},{2,0},{13,10},{9,6... | collective-permute-start | bytes 1179656 | tf_op jit(solution)/shard_map/ppermute | solution.py:377
  13.0 0.0 collective-permute-start.3
  13.0 10.9 %collective-permute-done.4.refs_2_ = bf16[12,128,128]{2,1,0:T(8,128)(2,1)S(1)} collective-permute-done((bf16[12,128,128]{2,1,0:T(8,128)(2,1)S(1)}, bf16[12,128,128]{2,1,0:T(8,128)(2,1)S(1)}, u32[]{:S(2)}, u32[]{:S(2)}) %collective-permute-start.4) | collective-permute-done | bytes 393248 | tf_op jit(solution)/shard_map/ppermute | solution.py:377
  23.8 0.5 whiten_hour.5.refs_0_
  24.4 0.1 collective-permute-start.7
  24.4 7.7 %collective-permute-done.10.refs_2_ = bf16[12,128,128]{2,1,0:T(8,128)(2,1)S(1)} collective-permute-done((bf16[12,128,128]{2,1,0:T(8,128)(2,1)S(1)}, bf16[12,128,128]{2,1,0:T(8,128)(2,1)S(1)}, u32[]{:S(2)}, u32[]{:S(2)}) %collective-permute-start.10) | collective-permute-done | bytes 393248 | tf_op jit(solution)/shard_map/ppermute | solution.py:377
  32.1 1.1 %collective-permute-start = (bf16[12,128,128]{2,1,0:T(8,128)(2,1)S(1)}, bf16[12,128,128]{2,1,0:T(8,128)(2,1)S(1)}, u32[]{:S(2)}, u32[]{:S(2)}) collective-permute-start(bf16[12,128,128]{2,1,0:T(8,128)(2,1)S(1)} %whiten_hour.3.refs_0_), channel_id=1, source_target_pairs={{15,14},{11,10},{7,6},{3,2},{13,12},{9,8},{5,4},{1,0},{14,11},{10,... | collective-permute-start | bytes 1179656 | tf_op jit(solution)/shard_map/ppermute | solution.py:377
  33.3 6.6 %collective-permute-done.1.refs_2_ = bf16[12,128,128]{2,1,0:T(8,128)(2,1)S(1)} collective-permute-done((bf16[12,128,128]{2,1,0:T(8,128)(2,1)S(1)}, bf16[12,128,128]{2,1,0:T(8,128)(2,1)S(1)}, u32[]{:S(2)}, u32[]{:S(2)}) %collective-permute-start.1) | collective-permute-done | bytes 393248 | tf_op jit(solution)/shard_map/ppermute | solution.py:377
  39.8 0.0 collective-permute-start.2
  39.8 0.5 collective-permute-start.9
  40.4 1.4 %collective-permute-start.11 = (bf16[12,128,128]{2,1,0:T(8,128)(2,1)S(1)}, bf16[12,128,128]{2,1,0:T(8,128)(2,1)S(1)}, u32[]{:S(2)}, u32[]{:S(2)}) collective-permute-start(bf16[12,128,128]{2,1,0:T(8,128)(2,1)S(1)} %collective-permute-done.10.refs_2_), channel_id=1, source_target_pairs={{0,1},{4,5},{8,9},{12,13},{1,0},{5,4},{9,8},{13,12},{2,3},{6,7},{1... | collective-permute-start | bytes 1179656 | tf_op jit(solution)/shard_map/ppermute | solution.py:377
  41.8 1.6 %pair_hour.2.refs_4_ = f32[2048,128]{1,0:T(8,128)S(1)} custom-call(bf16[12,128,128]{2,1,0:T(8,128)(2,1)S(1)} %whiten_hour.4.refs_0_, bf16[12,128,128]{2,1,0:T(8,128)(2,1)S(1)} %collective-permute-done.3.refs_1_, bf16[12,128,128]{2,1,0:T(8,128)(2,1)S(1)} %collective-permute-done.4.refs_2_, bf16[12,128,128]{2,1,0:T(8,128)(2,1)S(1)} %collective-permute-done.5.refs_3_), custom_call_target="tpu_custom_call" | custom-call | flops 3000000000 | bytes 12000000 | tf_op jit(solution)/shard_map/pair_hour/pallas_call | solution.py:308
  43.3 0.1 collective-permute-start.6
  43.4 1.7 %collective-permute-start.8 = (bf16[12,128,128]{2,1,0:T(8,128)(2,1)S(1)}, bf16[12,128,128]{2,1,0:T(8,128)(2,1)S(1)}, u32[]{:S(2)}, u32[]{:S(2)}) collective-permute-start(bf16[12,128,128]{2,1,0:T(8,128)(2,1)S(1)} %collective-permute-done.7.refs_2_), channel_id=1, source_target_pairs={{0,1},{4,5},{8,9},{12,13},{1,0},{5,4},{9,8},{13,12},{2,3},{6,7},{1... | collective-permute-start | bytes 1179656 | tf_op jit(solution)/shard_map/ppermute | solution.py:377
  45.1 2.4 %pair_hour_last.2 = (f32[4,288,128]{2,1,0:T(8,128)S(1)}, bf16[288,128]{1,0:T(8,128)(2,1)S(1)}, bf16[288,128]{1,0:T(8,128)(2,1)S(1)}, bf16[288,128]{1,0:T(8,128)(2,1)S(1)}) custom-call(bf16[12,128,128]{2,1,0:T(8,128)(2,1)S(1)} %whiten_hour.3.refs_0_, bf16[12,128,128]{2,1,0:T(8,128)(2,1)S(1)} %collective-permute-done.refs_1_, ...), custom_call_target="tpu_custom_call" | custom-call | flops 3000000000 | bytes 12000000 | tf_op jit(solution)/shard_map/pair_hour_last/pallas_call | solution.py:308
  47.5 0.1 collective-permute-start.15
  47.6 1.5 %collective-permute-done.9.refs_1_ = bf16[12,128,128]{2,1,0:T(8,128)(2,1)S(1)} collective-permute-done((bf16[12,128,128]{2,1,0:T(8,128)(2,1)S(1)}, bf16[12,128,128]{2,1,0:T(8,128)(2,1)S(1)}, u32[]{:S(2)}, u32[]{:S(2)}) %collective-permute-start.9) | collective-permute-done | bytes 393248 | tf_op jit(solution)/shard_map/ppermute | solution.py:377
  49.1 1.1 %collective-permute-start.17 = (bf16[288,128]{1,0:T(8,128)(2,1)S(1)}, bf16[288,128]{1,0:T(8,128)(2,1)S(1)}, u32[]{:S(2)}, u32[]{:S(2)}) collective-permute-start(bf16[288,128]{1,0:T(8,128)(2,1)S(1)} %get-tuple-element.28), channel_id=1, source_target_pairs={{0,3},{1,4},{2,5},{3,6},{4,7},{5,8},{6,9},{7,10},{8,11},{9,12},{10... | collective-permute-start | bytes 221192 | tf_op jit(solution)/shard_map/ppermute | solution.py:382
  50.3 1.6 %pair_hour.3.refs_4_ = f32[2048,128]{1,0:T(8,128)S(1)} custom-call(bf16[12,128,128]{2,1,0:T(8,128)(2,1)S(1)} %get-tuple-element.21.refs_0_, bf16[12,128,128]{2,1,0:T(8,128)(2,1)S(1)} %collective-permute-done.9.refs_1_, bf16[12,128,128]{2,1,0:T(8,128)(2,1)S(1)} %collective-permute-done.10.refs_2_, bf16[12,128,128]{2,1,0:T(8,128)(2,1)S(1)} %collective-permute-done.11.refs_3_), custom_call_target="tpu_custom_call" | custom-call | flops 3000000000 | bytes 12000000 | tf_op jit(solution)/shard_map/pair_hour/pallas_call | solution.py:308
  51.8 1.5 %collective-permute-done.6.refs_1_ = bf16[12,128,128]{2,1,0:T(8,128)(2,1)S(1)} collective-permute-done((bf16[12,128,128]{2,1,0:T(8,128)(2,1)S(1)}, bf16[12,128,128]{2,1,0:T(8,128)(2,1)S(1)}, u32[]{:S(2)}, u32[]{:S(2)}) %collective-permute-start.6) | collective-permute-done | bytes 393248 | tf_op jit(solution)/shard_map/ppermute | solution.py:377
  53.3 2.4 %pair_hour_last.3 = (f32[4,288,128]{2,1,0:T(8,128)S(1)}, bf16[288,128]{1,0:T(8,128)(2,1)S(1)}, bf16[288,128]{1,0:T(8,128)(2,1)S(1)}, bf16[288,128]{1,0:T(8,128)(2,1)S(1)}) custom-call(bf16[12,128,128]{2,1,0:T(8,128)(2,1)S(1)} %whiten_hour.5.refs_0_, bf16[12,128,128]{2,1,0:T(8,128)(2,1)S(1)} %collective-permute-done.6.refs_1_, ...), custom_call_target="tpu_custom_call" | custom-call | flops 3000000000 | bytes 12000000 | tf_op jit(solution)/shard_map/pair_hour_last/pallas_call | solution.py:308
  55.8 1.8 %collective-permute-start.12 = (bf16[288,128]{1,0:T(8,128)(2,1)S(1)}, bf16[288,128]{1,0:T(8,128)(2,1)S(1)}, u32[]{:S(2)}, u32[]{:S(2)}) collective-permute-start(bf16[288,128]{1,0:T(8,128)(2,1)S(1)} %get-tuple-element.22), channel_id=1, source_target_pairs={{0,15},{1,0},{2,1},{3,2},{4,3},{5,4},{6,5},{7,6},{8,7},{9,8},{10,9... | collective-permute-start | bytes 221192 | tf_op jit(solution)/shard_map/ppermute | solution.py:382
  57.6 1.2 %collective-permute-start.13 = (bf16[288,128]{1,0:T(8,128)(2,1)S(1)}, bf16[288,128]{1,0:T(8,128)(2,1)S(1)}, u32[]{:S(2)}, u32[]{:S(2)}) collective-permute-start(bf16[288,128]{1,0:T(8,128)(2,1)S(1)} %get-tuple-element.23), channel_id=1, source_target_pairs={{0,14},{1,15},{2,0},{3,1},{4,2},{5,3},{6,4},{7,5},{8,6},{9,7},{10,... | collective-permute-start | bytes 221192 | tf_op jit(solution)/shard_map/ppermute | solution.py:382
  58.8 0.7 %collective-permute-start.14 = (bf16[288,128]{1,0:T(8,128)(2,1)S(1)}, bf16[288,128]{1,0:T(8,128)(2,1)S(1)}, u32[]{:S(2)}, u32[]{:S(2)}) collective-permute-start(bf16[288,128]{1,0:T(8,128)(2,1)S(1)} %get-tuple-element.24), channel_id=1, source_target_pairs={{0,13},{1,14},{2,15},{3,0},{4,1},{5,2},{6,3},{7,4},{8,5},{9,6},{10... | collective-permute-start | bytes 221192 | tf_op jit(solution)/shard_map/ppermute | solution.py:382
  59.4 0.9 %join_below.1.refs_3_ = bf16[7,144,2,128]{3,2,1,0:T(2,128)(2,1)} custom-call(f32[4,288,128]{2,1,0:T(8,128)S(1)} %get-tuple-element.25.behind_ref, f32[4,288,128]{2,1,0:T(8,128)S(1)} %get-tuple-element.20.ahead_ref, bf16[288,128]{1,0:T(8,128)(2,1)S(1)} %collective-permute-done.15.refs_0_, bf16[288,128]{1,0:T(8,128)(2,1)S(1)} %collective-permute-done.16.refs_1_, ...), custom_call_target="tpu_custom_call" | custom-call | tf_op jit(solution)/shard_map/join_below/pallas_call | solution.py:343
  60.4 1.8 %collective-permute-done.13.refs_1_ = bf16[288,128]{1,0:T(8,128)(2,1)S(1)} collective-permute-done((bf16[288,128]{1,0:T(8,128)(2,1)S(1)}, bf16[288,128]{1,0:T(8,128)(2,1)S(1)}, u32[]{:S(2)}, u32[]{:S(2)}) %collective-permute-start.13) | collective-permute-done | bytes 73760 | tf_op jit(solution)/shard_map/ppermute | solution.py:382
  62.1 0.6 collective-permute-done.14.refs_2_
  62.8 0.9 %join_above.1 = bf16[7,144,2,128]{3,2,1,0:T(2,128)(2,1)} custom-call(f32[4,288,128]{2,1,0:T(8,128)S(1)} %get-tuple-element.20.ahead_ref, bf16[288,128]{1,0:T(8,128)(2,1)S(1)} %collective-permute-done.12.refs_0_, bf16[288,128]{1,0:T(8,128)(2,1)S(1)} %collective-permute-done.13.refs_1_, ...), custom_call_target="tpu_custom_call", output_to_operand_aliasing={{}: (4, {})} | custom-call | tf_op jit(solution)/shard_map/join_above/pallas_call | solution.py:352
  (14 shorter events, 0.0 us)
Async XLA Ops:
  2.4 21.5 %collective-permute-start.4 = (bf16[12,128,128]{2,1,0:T(8,128)(2,1)S(1)}, bf16[12,128,128]{2,1,0:T(8,128)(2,1)S(1)}, u32[]{:S(2)}, u32[]{:S(2)}) collective-permute-start(bf16[12,128,128]{2,1,0:T(8,128)(2,1)S(1)} %whiten_hour.4.refs_0_), channel_id=1, source_target_pairs={{15,13},{11,9},{7,5},{3,1},{14,12},{10,8},{6,4},{2,0},{13,10},{9,6... | collective-permute-start | bytes 1179656 | tf_op jit(solution)/shard_map/ppermute | solution.py:377
  7.9 24.2 %collective-permute-start.10 = (bf16[12,128,128]{2,1,0:T(8,128)(2,1)S(1)}, bf16[12,128,128]{2,1,0:T(8,128)(2,1)S(1)}, u32[]{:S(2)}, u32[]{:S(2)}) collective-permute-start(bf16[12,128,128]{2,1,0:T(8,128)(2,1)S(1)} %get-tuple-element.21.refs_0_), channel_id=1, source_target_pairs={{0,2},{4,6},{8,10},{12,14},{1,3},{5,7},{9,11},{13,15},{2,5},{6,9},... | collective-permute-start | bytes 1179656 | tf_op jit(solution)/shard_map/ppermute | solution.py:377
  8.4 31.4 %collective-permute-start.1 = (bf16[12,128,128]{2,1,0:T(8,128)(2,1)S(1)}, bf16[12,128,128]{2,1,0:T(8,128)(2,1)S(1)}, u32[]{:S(2)}, u32[]{:S(2)}) collective-permute-start(bf16[12,128,128]{2,1,0:T(8,128)(2,1)S(1)} %whiten_hour.3.refs_0_), channel_id=1, source_target_pairs={{15,13},{11,9},{7,5},{3,1},{14,12},{10,8},{6,4},{2,0},{13,10},{9,6... | collective-permute-start | bytes 1179656 | tf_op jit(solution)/shard_map/ppermute | solution.py:377
  13.0 26.9 %collective-permute-start.3 = (bf16[12,128,128]{2,1,0:T(8,128)(2,1)S(1)}, bf16[12,128,128]{2,1,0:T(8,128)(2,1)S(1)}, u32[]{:S(2)}, u32[]{:S(2)}) collective-permute-start(bf16[12,128,128]{2,1,0:T(8,128)(2,1)S(1)} %whiten_hour.4.refs_0_), channel_id=1, source_target_pairs={{15,14},{11,10},{7,6},{3,2},{13,12},{9,8},{5,4},{1,0},{14,11},{10,... | collective-permute-start | bytes 1179656 | tf_op jit(solution)/shard_map/ppermute | solution.py:377
  23.8 16.5 %collective-permute-start.5 = (bf16[12,128,128]{2,1,0:T(8,128)(2,1)S(1)}, bf16[12,128,128]{2,1,0:T(8,128)(2,1)S(1)}, u32[]{:S(2)}, u32[]{:S(2)}) collective-permute-start(bf16[12,128,128]{2,1,0:T(8,128)(2,1)S(1)} %collective-permute-done.4.refs_2_), channel_id=1, source_target_pairs={{15,14},{11,10},{7,6},{3,2},{14,15},{10,11},{6,7},{2,3},{13,12},{9... | collective-permute-start | bytes 1179656 | tf_op jit(solution)/shard_map/ppermute | solution.py:377
  24.4 19.0 %collective-permute-start.7 = (bf16[12,128,128]{2,1,0:T(8,128)(2,1)S(1)}, bf16[12,128,128]{2,1,0:T(8,128)(2,1)S(1)}, u32[]{:S(2)}, u32[]{:S(2)}) collective-permute-start(bf16[12,128,128]{2,1,0:T(8,128)(2,1)S(1)} %whiten_hour.5.refs_0_), channel_id=1, source_target_pairs={{0,2},{4,6},{8,10},{12,14},{1,3},{5,7},{9,11},{13,15},{2,5},{6,9},... | collective-permute-start | bytes 1179656 | tf_op jit(solution)/shard_map/ppermute | solution.py:377
  32.1 11.3 %collective-permute-start = (bf16[12,128,128]{2,1,0:T(8,128)(2,1)S(1)}, bf16[12,128,128]{2,1,0:T(8,128)(2,1)S(1)}, u32[]{:S(2)}, u32[]{:S(2)}) collective-permute-start(bf16[12,128,128]{2,1,0:T(8,128)(2,1)S(1)} %whiten_hour.3.refs_0_), channel_id=1, source_target_pairs={{15,14},{11,10},{7,6},{3,2},{13,12},{9,8},{5,4},{1,0},{14,11},{10,... | collective-permute-start | bytes 1179656 | tf_op jit(solution)/shard_map/ppermute | solution.py:377
  39.8 5.2 %collective-permute-start.2 = (bf16[12,128,128]{2,1,0:T(8,128)(2,1)S(1)}, bf16[12,128,128]{2,1,0:T(8,128)(2,1)S(1)}, u32[]{:S(2)}, u32[]{:S(2)}) collective-permute-start(bf16[12,128,128]{2,1,0:T(8,128)(2,1)S(1)} %collective-permute-done.1.refs_2_), channel_id=1, source_target_pairs={{15,14},{11,10},{7,6},{3,2},{14,15},{10,11},{6,7},{2,3},{13,12},{9... | collective-permute-start | bytes 1179656 | tf_op jit(solution)/shard_map/ppermute | solution.py:377
  39.8 9.3 %collective-permute-start.9 = (bf16[12,128,128]{2,1,0:T(8,128)(2,1)S(1)}, bf16[12,128,128]{2,1,0:T(8,128)(2,1)S(1)}, u32[]{:S(2)}, u32[]{:S(2)}) collective-permute-start(bf16[12,128,128]{2,1,0:T(8,128)(2,1)S(1)} %get-tuple-element.21.refs_0_), channel_id=1, source_target_pairs={{0,1},{4,5},{8,9},{12,13},{2,3},{6,7},{10,11},{14,15},{1,4},{5,8},... | collective-permute-start | bytes 1179656 | tf_op jit(solution)/shard_map/ppermute | solution.py:377
  40.4 8.8 %collective-permute-start.11 = (bf16[12,128,128]{2,1,0:T(8,128)(2,1)S(1)}, bf16[12,128,128]{2,1,0:T(8,128)(2,1)S(1)}, u32[]{:S(2)}, u32[]{:S(2)}) collective-permute-start(bf16[12,128,128]{2,1,0:T(8,128)(2,1)S(1)} %collective-permute-done.10.refs_2_), channel_id=1, source_target_pairs={{0,1},{4,5},{8,9},{12,13},{1,0},{5,4},{9,8},{13,12},{2,3},{6,7},{1... | collective-permute-start | bytes 1179656 | tf_op jit(solution)/shard_map/ppermute | solution.py:377
  43.3 10.0 %collective-permute-start.6 = (bf16[12,128,128]{2,1,0:T(8,128)(2,1)S(1)}, bf16[12,128,128]{2,1,0:T(8,128)(2,1)S(1)}, u32[]{:S(2)}, u32[]{:S(2)}) collective-permute-start(bf16[12,128,128]{2,1,0:T(8,128)(2,1)S(1)} %whiten_hour.5.refs_0_), channel_id=1, source_target_pairs={{0,1},{4,5},{8,9},{12,13},{2,3},{6,7},{10,11},{14,15},{1,4},{5,8},... | collective-permute-start | bytes 1179656 | tf_op jit(solution)/shard_map/ppermute | solution.py:377
  43.4 9.9 %collective-permute-start.8 = (bf16[12,128,128]{2,1,0:T(8,128)(2,1)S(1)}, bf16[12,128,128]{2,1,0:T(8,128)(2,1)S(1)}, u32[]{:S(2)}, u32[]{:S(2)}) collective-permute-start(bf16[12,128,128]{2,1,0:T(8,128)(2,1)S(1)} %collective-permute-done.7.refs_2_), channel_id=1, source_target_pairs={{0,1},{4,5},{8,9},{12,13},{1,0},{5,4},{9,8},{13,12},{2,3},{6,7},{1... | collective-permute-start | bytes 1179656 | tf_op jit(solution)/shard_map/ppermute | solution.py:377
  47.5 11.3 %collective-permute-start.15 = (bf16[288,128]{1,0:T(8,128)(2,1)S(1)}, bf16[288,128]{1,0:T(8,128)(2,1)S(1)}, u32[]{:S(2)}, u32[]{:S(2)}) collective-permute-start(bf16[288,128]{1,0:T(8,128)(2,1)S(1)} %get-tuple-element.26), channel_id=1, source_target_pairs={{0,1},{1,2},{2,3},{3,4},{4,5},{5,6},{6,7},{7,8},{8,9},{9,10},{10,1... | collective-permute-start | bytes 221192 | tf_op jit(solution)/shard_map/ppermute | solution.py:382
  49.1 10.3 %collective-permute-start.16 = (bf16[288,128]{1,0:T(8,128)(2,1)S(1)}, bf16[288,128]{1,0:T(8,128)(2,1)S(1)}, u32[]{:S(2)}, u32[]{:S(2)}) collective-permute-start(bf16[288,128]{1,0:T(8,128)(2,1)S(1)} %get-tuple-element.27), channel_id=1, source_target_pairs={{0,2},{1,3},{2,4},{3,5},{4,6},{5,7},{6,8},{7,9},{8,10},{9,11},{10,... | collective-permute-start | bytes 221192 | tf_op jit(solution)/shard_map/ppermute | solution.py:382
  49.1 10.3 %collective-permute-start.17 = (bf16[288,128]{1,0:T(8,128)(2,1)S(1)}, bf16[288,128]{1,0:T(8,128)(2,1)S(1)}, u32[]{:S(2)}, u32[]{:S(2)}) collective-permute-start(bf16[288,128]{1,0:T(8,128)(2,1)S(1)} %get-tuple-element.28), channel_id=1, source_target_pairs={{0,3},{1,4},{2,5},{3,6},{4,7},{5,8},{6,9},{7,10},{8,11},{9,12},{10... | collective-permute-start | bytes 221192 | tf_op jit(solution)/shard_map/ppermute | solution.py:382
  55.8 4.6 %collective-permute-start.12 = (bf16[288,128]{1,0:T(8,128)(2,1)S(1)}, bf16[288,128]{1,0:T(8,128)(2,1)S(1)}, u32[]{:S(2)}, u32[]{:S(2)}) collective-permute-start(bf16[288,128]{1,0:T(8,128)(2,1)S(1)} %get-tuple-element.22), channel_id=1, source_target_pairs={{0,15},{1,0},{2,1},{3,2},{4,3},{5,4},{6,5},{7,6},{8,7},{9,8},{10,9... | collective-permute-start | bytes 221192 | tf_op jit(solution)/shard_map/ppermute | solution.py:382
  57.6 4.5 %collective-permute-start.13 = (bf16[288,128]{1,0:T(8,128)(2,1)S(1)}, bf16[288,128]{1,0:T(8,128)(2,1)S(1)}, u32[]{:S(2)}, u32[]{:S(2)}) collective-permute-start(bf16[288,128]{1,0:T(8,128)(2,1)S(1)} %get-tuple-element.23), channel_id=1, source_target_pairs={{0,14},{1,15},{2,0},{3,1},{4,2},{5,3},{6,4},{7,5},{8,6},{9,7},{10,... | collective-permute-start | bytes 221192 | tf_op jit(solution)/shard_map/ppermute | solution.py:382
  58.8 4.0 %collective-permute-start.14 = (bf16[288,128]{1,0:T(8,128)(2,1)S(1)}, bf16[288,128]{1,0:T(8,128)(2,1)S(1)}, u32[]{:S(2)}, u32[]{:S(2)}) collective-permute-start(bf16[288,128]{1,0:T(8,128)(2,1)S(1)} %get-tuple-element.24), channel_id=1, source_target_pairs={{0,13},{1,14},{2,15},{3,0},{4,1},{5,2},{6,3},{7,4},{8,5},{9,6},{10... | collective-permute-start | bytes 221192 | tf_op jit(solution)/shard_map/ppermute | solution.py:382

commit v4 on v3

--- a/solution.py
+++ b/solution.py
@@ -10,13 +10,11 @@
 
 
 ROUNDS = 3
-COMPONENTS = 3
 LANES = 128
 PITCH = 16
 SKEW = 8
 MIB = 1 << 20
 PAIR_LIMIT = 10 * MIB
-FETCHES = COMPONENTS
 PAIR_COST = pl.CostEstimate(flops=3_000_000_000, transcendentals=0, bytes_accessed=12_000_000)
 WHITEN_COST = pl.CostEstimate(flops=2_000_000_000, transcendentals=0, bytes_accessed=8_000_000)
 
@@ -88,7 +86,7 @@
 
 
 def whiten_first_kernel(counts_hbm, records_hbm, gap_hbm, table_hbm, *refs):
-    out_ref, rest_ref, valid_ref, table_ref, counts_ref, records_ref, gap_ref, sems = refs
+    out_ref, valid_ref, table_ref, counts_ref, records_ref, gap_ref, sems = refs
     seg_hour = records_ref.shape[1]
     hours = valid_ref.shape[0]
 
@@ -105,24 +103,19 @@
 
     moves = list(parts(0, records_ref, channels))
     moves += [(counts_hbm, counts_ref), (gap_hbm, gap_ref), (table_hbm, table_ref)]
-    now = len(moves)
-    for hour in range(1, hours):
-        moves += parts(hour, rest_ref.at[hour - 1], FETCHES)
     copies = [
         pltpu.make_async_copy(source, target, sems.at[i])
         for i, (source, target) in enumerate(moves)
     ]
     for copy in copies:
         copy.start()
-    for copy in copies[:now]:
+    for copy in copies:
         copy.wait()
     valid = [validity_rows(hour, seg_hour, counts_ref, gap_ref) for hour in range(hours)]
     for hour in range(1, hours):
         for station, row in enumerate(valid[hour]):
             valid_ref[hour, station : station + 1, :] = row
     whiten_block(records_ref, valid[0], table_ref, out_ref)
-    for copy in copies[now:]:
-        copy.wait()
 
 
 def whiten_first(records, counts, gap_mask, table):
@@ -136,17 +129,16 @@
         whiten_first_kernel,
         out_shape=[
             jax.ShapeDtypeStruct((channels, samples // 2, LANES), jnp.bfloat16),
-            jax.ShapeDtypeStruct((hours - 1, *block), records.dtype),
             jax.ShapeDtypeStruct((hours, stations, LANES), jnp.float32),
             jax.ShapeDtypeStruct(table.shape, table.dtype),
         ],
         in_specs=[hbm] * 4,
-        out_specs=[vmem] * 4,
+        out_specs=[vmem] * 3,
         scratch_shapes=[
             pltpu.SMEM(counts.shape, counts.dtype),
             pltpu.VMEM(block, records.dtype),
             pltpu.VMEM(gap_mask.shape, gap_mask.dtype),
-            pltpu.SemaphoreType.DMA((channels + 3 + (hours - 1) * FETCHES,)),
+            pltpu.SemaphoreType.DMA((channels + 3,)),
         ],
         cost_estimate=WHITEN_COST,
         compiler_params=pltpu.CompilerParams(vmem_limit_bytes=4 * MIB),
@@ -159,13 +151,14 @@
     )
 
 
-def whiten_hour_kernel(hour, rest_ref, valid_ref, table_ref, out_ref):
+def whiten_hour_kernel(hour, records_ref, valid_ref, table_ref, out_ref):
     valid = [valid_ref[hour, station : station + 1, :] for station in range(valid_ref.shape[1])]
-    whiten_block(rest_ref.at[hour - 1], valid, table_ref, out_ref)
-
-
-def whiten_hour(rest, valid, table, hour):
-    _, channels, _, samples = rest.shape
+    seg_hour = out_ref.shape[2] // 2
+    whiten_block(records_ref.at[:, pl.ds(hour * seg_hour, seg_hour), :], valid, table_ref, out_ref)
+
+
+def whiten_hour(records, valid, table, hour):
+    channels, _, samples = records.shape
     vmem = pl.BlockSpec(memory_space=pltpu.VMEM)
     return pl.pallas_call(
         lambda *refs: whiten_hour_kernel(hour, *refs),
@@ -175,7 +168,7 @@
         cost_estimate=WHITEN_COST,
         compiler_params=pltpu.CompilerParams(vmem_limit_bytes=4 * MIB),
         name="whiten_hour",
-    )(rest, valid, table)
+    )(records, valid, table)
 
 
 def pair_hour_kernel(hours, first, last, mirrored, *refs):
@@ -414,8 +407,8 @@
     bins = samples // 2
     count = lax.axis_size("sta")
     table = fourier_matrix(samples)
-    first, rest, valid, table = whiten_first(records, counts, gap_mask, table)
-    whitened = [first] + [whiten_hour(rest, valid, table, hour) for hour in range(1, hours)]
+    first, valid, table = whiten_first(records, counts, gap_mask, table)
+    whitened = [first] + [whiten_hour(records, valid, table, hour) for hour in range(1, hours)]
     partners = [fetch_partners(whitened[hour], count, hour) for hour in range(hours)]
     sums = [None, None]
     for hour in range(hours):

time: 64 us -> 64 us (level)
  no operation moved by 1% of the time
where the time goes in v4:
time: 64 us; the launch traced here: 63.6 us
  waiting for transfers between devices  30.6 us (48%)
  starting transfers between devices  19.7 us (31%)
  Pallas kernels  13.2 us (21%)
    ppermute x12, waiting for transfers between devices, send(): return lax.ppermute(value, 'sta', pairs)  28.2 us
    ppermute x12, starting transfers between devices, send(): return lax.ppermute(value, 'sta', pairs)  14.9 us
    pallas_call x4, Pallas kernels, pair_hour(): pl.pallas_call(lambda *refs: pair_hour_kernel(hours, first, last, mirrore...  7.97 us
    ppermute x6, starting transfers between devices, shift(): return lax.ppermute(value, 'sta', pairs)  4.88 us
    ppermute x6, waiting for transfers between devices, shift(): return lax.ppermute(value, 'sta', pairs)  2.37 us
    pallas_call x1, Pallas kernels, whiten_first(): pl.pallas_call(whiten_first_kernel, out_shape=[jax.ShapeDtypeStruct((chan...  1.86 us
    pallas_call x3, Pallas kernels, whiten_hour(): pl.pallas_call(lambda *refs: whiten_hour_kernel(hour, *refs), out_shape=j...  1.53 us
  transfers between devices with their start and end apart: 18, of which 7 were waited for; matrix products, arithmetic and copies ran while one was open for 0% of the time, Pallas kernels for 16%

profile of v4, /device:TPU:0, one launch (start us, length us, event | category | flops | bytes accessed | tf_op | source)
XLA Modules:
  0.0 63.6 jit_solution(3902332286836235284)
XLA Ops:
  0.0 1.9 %whiten_first.1 = (bf16[12,128,128]{2,1,0:T(8,128)(2,1)S(1)}, f32[4,4,128]{2,1,0:T(4,128)S(1)}, bf16[256,256]{1,0:T(8,128)(2,1)S(1)}) custom-call(s32[4,4]{1,0:T(4,128)} %counts_hbm.1, bf16[12,256,256]{2,1,0:T(8,128)(2,1)} %refs_0_.5, s32[4,256]{1,0:T(4,128)} %gap_hbm.1, bf16[256,256]{1,0:T(8,128)(2,1)} %constant.2.clone.table_hbm), custom_call_target="tpu_custom_call" | custom-call | flops 2000000000 | bytes 8000000 | tf_op jit(solution)/shard_map/whiten_first/pallas_call | solution.py:128
  1.9 0.5 whiten_hour.4.refs_0_
  2.4 5.5 %collective-permute-start.4 = (bf16[12,128,128]{2,1,0:T(8,128)(2,1)S(1)}, bf16[12,128,128]{2,1,0:T(8,128)(2,1)S(1)}, u32[]{:S(2)}, u32[]{:S(2)}) collective-permute-start(bf16[12,128,128]{2,1,0:T(8,128)(2,1)S(1)} %whiten_hour.4.refs_0_), channel_id=1, source_target_pairs={{15,13},{11,9},{7,5},{3,1},{14,12},{10,8},{6,4},{2,0},{13,10},{9,6... | collective-permute-start | bytes 1179656 | tf_op jit(solution)/shard_map/ppermute | solution.py:370
  7.9 0.0 collective-permute-start.10
  7.9 0.5 whiten_hour.3.refs_0_
  8.5 4.5 %collective-permute-start.1 = (bf16[12,128,128]{2,1,0:T(8,128)(2,1)S(1)}, bf16[12,128,128]{2,1,0:T(8,128)(2,1)S(1)}, u32[]{:S(2)}, u32[]{:S(2)}) collective-permute-start(bf16[12,128,128]{2,1,0:T(8,128)(2,1)S(1)} %whiten_hour.3.refs_0_), channel_id=1, source_target_pairs={{15,13},{11,9},{7,5},{3,1},{14,12},{10,8},{6,4},{2,0},{13,10},{9,6... | collective-permute-start | bytes 1179656 | tf_op jit(solution)/shard_map/ppermute | solution.py:370
  13.0 10.9 %collective-permute-done.4.refs_2_ = bf16[12,128,128]{2,1,0:T(8,128)(2,1)S(1)} collective-permute-done((bf16[12,128,128]{2,1,0:T(8,128)(2,1)S(1)}, bf16[12,128,128]{2,1,0:T(8,128)(2,1)S(1)}, u32[]{:S(2)}, u32[]{:S(2)}) %collective-permute-start.4) | collective-permute-done | bytes 393248 | tf_op jit(solution)/shard_map/ppermute | solution.py:370
  23.9 0.0 collective-permute-start.5
  23.9 0.5 whiten_hour.5.refs_0_
  24.4 0.1 collective-permute-start.7
  24.4 7.7 %collective-permute-done.10.refs_2_ = bf16[12,128,128]{2,1,0:T(8,128)(2,1)S(1)} collective-permute-done((bf16[12,128,128]{2,1,0:T(8,128)(2,1)S(1)}, bf16[12,128,128]{2,1,0:T(8,128)(2,1)S(1)}, u32[]{:S(2)}, u32[]{:S(2)}) %collective-permute-start.10) | collective-permute-done | bytes 393248 | tf_op jit(solution)/shard_map/ppermute | solution.py:370
  32.1 1.1 %collective-permute-start = (bf16[12,128,128]{2,1,0:T(8,128)(2,1)S(1)}, bf16[12,128,128]{2,1,0:T(8,128)(2,1)S(1)}, u32[]{:S(2)}, u32[]{:S(2)}) collective-permute-start(bf16[12,128,128]{2,1,0:T(8,128)(2,1)S(1)} %whiten_hour.3.refs_0_), channel_id=1, source_target_pairs={{15,14},{11,10},{7,6},{3,2},{13,12},{9,8},{5,4},{1,0},{14,11},{10,... | collective-permute-start | bytes 1179656 | tf_op jit(solution)/shard_map/ppermute | solution.py:370
  33.3 6.6 %collective-permute-done.1.refs_2_ = bf16[12,128,128]{2,1,0:T(8,128)(2,1)S(1)} collective-permute-done((bf16[12,128,128]{2,1,0:T(8,128)(2,1)S(1)}, bf16[12,128,128]{2,1,0:T(8,128)(2,1)S(1)}, u32[]{:S(2)}, u32[]{:S(2)}) %collective-permute-start.1) | collective-permute-done | bytes 393248 | tf_op jit(solution)/shard_map/ppermute | solution.py:370
  39.9 0.5 collective-permute-start.9
  40.4 1.4 %collective-permute-start.11 = (bf16[12,128,128]{2,1,0:T(8,128)(2,1)S(1)}, bf16[12,128,128]{2,1,0:T(8,128)(2,1)S(1)}, u32[]{:S(2)}, u32[]{:S(2)}) collective-permute-start(bf16[12,128,128]{2,1,0:T(8,128)(2,1)S(1)} %collective-permute-done.10.refs_2_), channel_id=1, source_target_pairs={{0,1},{4,5},{8,9},{12,13},{1,0},{5,4},{9,8},{13,12},{2,3},{6,7},{1... | collective-permute-start | bytes 1179656 | tf_op jit(solution)/shard_map/ppermute | solution.py:370
  41.8 1.6 %pair_hour.2.refs_4_ = f32[2048,128]{1,0:T(8,128)S(1)} custom-call(bf16[12,128,128]{2,1,0:T(8,128)(2,1)S(1)} %whiten_hour.4.refs_0_, bf16[12,128,128]{2,1,0:T(8,128)(2,1)S(1)} %collective-permute-done.3.refs_1_, bf16[12,128,128]{2,1,0:T(8,128)(2,1)S(1)} %collective-permute-done.4.refs_2_, bf16[12,128,128]{2,1,0:T(8,128)(2,1)S(1)} %collective-permute-done.5.refs_3_), custom_call_target="tpu_custom_call" | custom-call | flops 3000000000 | bytes 12000000 | tf_op jit(solution)/shard_map/pair_hour/pallas_call | solution.py:301
  43.3 0.1 collective-permute-start.6
  43.4 1.7 %collective-permute-start.8 = (bf16[12,128,128]{2,1,0:T(8,128)(2,1)S(1)}, bf16[12,128,128]{2,1,0:T(8,128)(2,1)S(1)}, u32[]{:S(2)}, u32[]{:S(2)}) collective-permute-start(bf16[12,128,128]{2,1,0:T(8,128)(2,1)S(1)} %collective-permute-done.7.refs_2_), channel_id=1, source_target_pairs={{0,1},{4,5},{8,9},{12,13},{1,0},{5,4},{9,8},{13,12},{2,3},{6,7},{1... | collective-permute-start | bytes 1179656 | tf_op jit(solution)/shard_map/ppermute | solution.py:370
  45.1 2.4 %pair_hour_last.2 = (f32[4,288,128]{2,1,0:T(8,128)S(1)}, bf16[288,128]{1,0:T(8,128)(2,1)S(1)}, bf16[288,128]{1,0:T(8,128)(2,1)S(1)}, bf16[288,128]{1,0:T(8,128)(2,1)S(1)}) custom-call(bf16[12,128,128]{2,1,0:T(8,128)(2,1)S(1)} %whiten_hour.3.refs_0_, bf16[12,128,128]{2,1,0:T(8,128)(2,1)S(1)} %collective-permute-done.refs_1_, ...), custom_call_target="tpu_custom_call" | custom-call | flops 3000000000 | bytes 12000000 | tf_op jit(solution)/shard_map/pair_hour_last/pallas_call | solution.py:301
  47.5 0.1 collective-permute-start.15
  47.6 1.5 %collective-permute-done.9.refs_1_ = bf16[12,128,128]{2,1,0:T(8,128)(2,1)S(1)} collective-permute-done((bf16[12,128,128]{2,1,0:T(8,128)(2,1)S(1)}, bf16[12,128,128]{2,1,0:T(8,128)(2,1)S(1)}, u32[]{:S(2)}, u32[]{:S(2)}) %collective-permute-start.9) | collective-permute-done | bytes 393248 | tf_op jit(solution)/shard_map/ppermute | solution.py:370
  49.1 1.1 %collective-permute-start.17 = (bf16[288,128]{1,0:T(8,128)(2,1)S(1)}, bf16[288,128]{1,0:T(8,128)(2,1)S(1)}, u32[]{:S(2)}, u32[]{:S(2)}) collective-permute-start(bf16[288,128]{1,0:T(8,128)(2,1)S(1)} %get-tuple-element.26), channel_id=1, source_target_pairs={{0,3},{1,4},{2,5},{3,6},{4,7},{5,8},{6,9},{7,10},{8,11},{9,12},{10... | collective-permute-start | bytes 221192 | tf_op jit(solution)/shard_map/ppermute | solution.py:375
  50.3 1.6 %pair_hour.3.refs_4_ = f32[2048,128]{1,0:T(8,128)S(1)} custom-call(bf16[12,128,128]{2,1,0:T(8,128)(2,1)S(1)} %get-tuple-element.19.refs_0_, bf16[12,128,128]{2,1,0:T(8,128)(2,1)S(1)} %collective-permute-done.9.refs_1_, bf16[12,128,128]{2,1,0:T(8,128)(2,1)S(1)} %collective-permute-done.10.refs_2_, bf16[12,128,128]{2,1,0:T(8,128)(2,1)S(1)} %collective-permute-done.11.refs_3_), custom_call_target="tpu_custom_call" | custom-call | flops 3000000000 | bytes 12000000 | tf_op jit(solution)/shard_map/pair_hour/pallas_call | solution.py:301
  51.8 1.5 %collective-permute-done.6.refs_1_ = bf16[12,128,128]{2,1,0:T(8,128)(2,1)S(1)} collective-permute-done((bf16[12,128,128]{2,1,0:T(8,128)(2,1)S(1)}, bf16[12,128,128]{2,1,0:T(8,128)(2,1)S(1)}, u32[]{:S(2)}, u32[]{:S(2)}) %collective-permute-start.6) | collective-permute-done | bytes 393248 | tf_op jit(solution)/shard_map/ppermute | solution.py:370
  53.3 2.4 %pair_hour_last.3 = (f32[4,288,128]{2,1,0:T(8,128)S(1)}, bf16[288,128]{1,0:T(8,128)(2,1)S(1)}, bf16[288,128]{1,0:T(8,128)(2,1)S(1)}, bf16[288,128]{1,0:T(8,128)(2,1)S(1)}) custom-call(bf16[12,128,128]{2,1,0:T(8,128)(2,1)S(1)} %whiten_hour.5.refs_0_, bf16[12,128,128]{2,1,0:T(8,128)(2,1)S(1)} %collective-permute-done.6.refs_1_, ...), custom_call_target="tpu_custom_call" | custom-call | flops 3000000000 | bytes 12000000 | tf_op jit(solution)/shard_map/pair_hour_last/pallas_call | solution.py:301
  55.8 1.8 %collective-permute-start.12 = (bf16[288,128]{1,0:T(8,128)(2,1)S(1)}, bf16[288,128]{1,0:T(8,128)(2,1)S(1)}, u32[]{:S(2)}, u32[]{:S(2)}) collective-permute-start(bf16[288,128]{1,0:T(8,128)(2,1)S(1)} %get-tuple-element.20), channel_id=1, source_target_pairs={{0,15},{1,0},{2,1},{3,2},{4,3},{5,4},{6,5},{7,6},{8,7},{9,8},{10,9... | collective-permute-start | bytes 221192 | tf_op jit(solution)/shard_map/ppermute | solution.py:375
  57.6 1.2 %collective-permute-start.13 = (bf16[288,128]{1,0:T(8,128)(2,1)S(1)}, bf16[288,128]{1,0:T(8,128)(2,1)S(1)}, u32[]{:S(2)}, u32[]{:S(2)}) collective-permute-start(bf16[288,128]{1,0:T(8,128)(2,1)S(1)} %get-tuple-element.21), channel_id=1, source_target_pairs={{0,14},{1,15},{2,0},{3,1},{4,2},{5,3},{6,4},{7,5},{8,6},{9,7},{10,... | collective-permute-start | bytes 221192 | tf_op jit(solution)/shard_map/ppermute | solution.py:375
  58.8 0.6 %collective-permute-start.14 = (bf16[288,128]{1,0:T(8,128)(2,1)S(1)}, bf16[288,128]{1,0:T(8,128)(2,1)S(1)}, u32[]{:S(2)}, u32[]{:S(2)}) collective-permute-start(bf16[288,128]{1,0:T(8,128)(2,1)S(1)} %get-tuple-element.22), channel_id=1, source_target_pairs={{0,13},{1,14},{2,15},{3,0},{4,1},{5,2},{6,3},{7,4},{8,5},{9,6},{10... | collective-permute-start | bytes 221192 | tf_op jit(solution)/shard_map/ppermute | solution.py:375
  59.5 0.9 %join_below.1.refs_3_ = bf16[7,144,2,128]{3,2,1,0:T(2,128)(2,1)} custom-call(f32[4,288,128]{2,1,0:T(8,128)S(1)} %get-tuple-element.23.behind_ref, f32[4,288,128]{2,1,0:T(8,128)S(1)} %get-tuple-element.18.ahead_ref, bf16[288,128]{1,0:T(8,128)(2,1)S(1)} %collective-permute-done.15.refs_0_, bf16[288,128]{1,0:T(8,128)(2,1)S(1)} %collective-permute-done.16.refs_1_, ...), custom_call_target="tpu_custom_call" | custom-call | tf_op jit(solution)/shard_map/join_below/pallas_call | solution.py:336
  60.4 1.8 %collective-permute-done.13.refs_1_ = bf16[288,128]{1,0:T(8,128)(2,1)S(1)} collective-permute-done((bf16[288,128]{1,0:T(8,128)(2,1)S(1)}, bf16[288,128]{1,0:T(8,128)(2,1)S(1)}, u32[]{:S(2)}, u32[]{:S(2)}) %collective-permute-start.13) | collective-permute-done | bytes 73760 | tf_op jit(solution)/shard_map/ppermute | solution.py:375
  62.2 0.6 collective-permute-done.14.refs_2_
  62.8 0.9 %join_above.1 = bf16[7,144,2,128]{3,2,1,0:T(2,128)(2,1)} custom-call(f32[4,288,128]{2,1,0:T(8,128)S(1)} %get-tuple-element.18.ahead_ref, bf16[288,128]{1,0:T(8,128)(2,1)S(1)} %collective-permute-done.12.refs_0_, bf16[288,128]{1,0:T(8,128)(2,1)S(1)} %collective-permute-done.13.refs_1_, ...), custom_call_target="tpu_custom_call", output_to_operand_aliasing={{}: (4, {})} | custom-call | tf_op jit(solution)/shard_map/join_above/pallas_call | solution.py:345
  (16 shorter events, 0.0 us)
Async XLA Ops:
  0.0 1.9 %copy-start = (bf16[12,256,256]{2,1,0:T(8,128)(2,1)S(1)}, bf16[12,256,256]{2,1,0:T(8,128)(2,1)}, u32[]{:S(2)}) copy-start(bf16[12,256,256]{2,1,0:T(8,128)(2,1)} %refs_0_.5) | copy-start | bytes 4718596
  2.4 21.5 %collective-permute-start.4 = (bf16[12,128,128]{2,1,0:T(8,128)(2,1)S(1)}, bf16[12,128,128]{2,1,0:T(8,128)(2,1)S(1)}, u32[]{:S(2)}, u32[]{:S(2)}) collective-permute-start(bf16[12,128,128]{2,1,0:T(8,128)(2,1)S(1)} %whiten_hour.4.refs_0_), channel_id=1, source_target_pairs={{15,13},{11,9},{7,5},{3,1},{14,12},{10,8},{6,4},{2,0},{13,10},{9,6... | collective-permute-start | bytes 1179656 | tf_op jit(solution)/shard_map/ppermute | solution.py:370
  7.9 24.2 %collective-permute-start.10 = (bf16[12,128,128]{2,1,0:T(8,128)(2,1)S(1)}, bf16[12,128,128]{2,1,0:T(8,128)(2,1)S(1)}, u32[]{:S(2)}, u32[]{:S(2)}) collective-permute-start(bf16[12,128,128]{2,1,0:T(8,128)(2,1)S(1)} %get-tuple-element.19.refs_0_), channel_id=1, source_target_pairs={{0,2},{4,6},{8,10},{12,14},{1,3},{5,7},{9,11},{13,15},{2,5},{6,9},... | collective-permute-start | bytes 1179656 | tf_op jit(solution)/shard_map/ppermute | solution.py:370
  8.5 31.4 %collective-permute-start.1 = (bf16[12,128,128]{2,1,0:T(8,128)(2,1)S(1)}, bf16[12,128,128]{2,1,0:T(8,128)(2,1)S(1)}, u32[]{:S(2)}, u32[]{:S(2)}) collective-permute-start(bf16[12,128,128]{2,1,0:T(8,128)(2,1)S(1)} %whiten_hour.3.refs_0_), channel_id=1, source_target_pairs={{15,13},{11,9},{7,5},{3,1},{14,12},{10,8},{6,4},{2,0},{13,10},{9,6... | collective-permute-start | bytes 1179656 | tf_op jit(solution)/shard_map/ppermute | solution.py:370
  13.0 26.9 %collective-permute-start.3 = (bf16[12,128,128]{2,1,0:T(8,128)(2,1)S(1)}, bf16[12,128,128]{2,1,0:T(8,128)(2,1)S(1)}, u32[]{:S(2)}, u32[]{:S(2)}) collective-permute-start(bf16[12,128,128]{2,1,0:T(8,128)(2,1)S(1)} %whiten_hour.4.refs_0_), channel_id=1, source_target_pairs={{15,14},{11,10},{7,6},{3,2},{13,12},{9,8},{5,4},{1,0},{14,11},{10,... | collective-permute-start | bytes 1179656 | tf_op jit(solution)/shard_map/ppermute | solution.py:370
  23.9 16.5 %collective-permute-start.5 = (bf16[12,128,128]{2,1,0:T(8,128)(2,1)S(1)}, bf16[12,128,128]{2,1,0:T(8,128)(2,1)S(1)}, u32[]{:S(2)}, u32[]{:S(2)}) collective-permute-start(bf16[12,128,128]{2,1,0:T(8,128)(2,1)S(1)} %collective-permute-done.4.refs_2_), channel_id=1, source_target_pairs={{15,14},{11,10},{7,6},{3,2},{14,15},{10,11},{6,7},{2,3},{13,12},{9... | collective-permute-start | bytes 1179656 | tf_op jit(solution)/shard_map/ppermute | solution.py:370
  24.4 19.0 %collective-permute-start.7 = (bf16[12,128,128]{2,1,0:T(8,128)(2,1)S(1)}, bf16[12,128,128]{2,1,0:T(8,128)(2,1)S(1)}, u32[]{:S(2)}, u32[]{:S(2)}) collective-permute-start(bf16[12,128,128]{2,1,0:T(8,128)(2,1)S(1)} %whiten_hour.5.refs_0_), channel_id=1, source_target_pairs={{0,2},{4,6},{8,10},{12,14},{1,3},{5,7},{9,11},{13,15},{2,5},{6,9},... | collective-permute-start | bytes 1179656 | tf_op jit(solution)/shard_map/ppermute | solution.py:370
  32.1 11.3 %collective-permute-start = (bf16[12,128,128]{2,1,0:T(8,128)(2,1)S(1)}, bf16[12,128,128]{2,1,0:T(8,128)(2,1)S(1)}, u32[]{:S(2)}, u32[]{:S(2)}) collective-permute-start(bf16[12,128,128]{2,1,0:T(8,128)(2,1)S(1)} %whiten_hour.3.refs_0_), channel_id=1, source_target_pairs={{15,14},{11,10},{7,6},{3,2},{13,12},{9,8},{5,4},{1,0},{14,11},{10,... | collective-permute-start | bytes 1179656 | tf_op jit(solution)/shard_map/ppermute | solution.py:370
  39.9 5.2 %collective-permute-start.2 = (bf16[12,128,128]{2,1,0:T(8,128)(2,1)S(1)}, bf16[12,128,128]{2,1,0:T(8,128)(2,1)S(1)}, u32[]{:S(2)}, u32[]{:S(2)}) collective-permute-start(bf16[12,128,128]{2,1,0:T(8,128)(2,1)S(1)} %collective-permute-done.1.refs_2_), channel_id=1, source_target_pairs={{15,14},{11,10},{7,6},{3,2},{14,15},{10,11},{6,7},{2,3},{13,12},{9... | collective-permute-start | bytes 1179656 | tf_op jit(solution)/shard_map/ppermute | solution.py:370
  39.9 9.3 %collective-permute-start.9 = (bf16[12,128,128]{2,1,0:T(8,128)(2,1)S(1)}, bf16[12,128,128]{2,1,0:T(8,128)(2,1)S(1)}, u32[]{:S(2)}, u32[]{:S(2)}) collective-permute-start(bf16[12,128,128]{2,1,0:T(8,128)(2,1)S(1)} %get-tuple-element.19.refs_0_), channel_id=1, source_target_pairs={{0,1},{4,5},{8,9},{12,13},{2,3},{6,7},{10,11},{14,15},{1,4},{5,8},... | collective-permute-start | bytes 1179656 | tf_op jit(solution)/shard_map/ppermute | solution.py:370
  40.4 8.8 %collective-permute-start.11 = (bf16[12,128,128]{2,1,0:T(8,128)(2,1)S(1)}, bf16[12,128,128]{2,1,0:T(8,128)(2,1)S(1)}, u32[]{:S(2)}, u32[]{:S(2)}) collective-permute-start(bf16[12,128,128]{2,1,0:T(8,128)(2,1)S(1)} %collective-permute-done.10.refs_2_), channel_id=1, source_target_pairs={{0,1},{4,5},{8,9},{12,13},{1,0},{5,4},{9,8},{13,12},{2,3},{6,7},{1... | collective-permute-start | bytes 1179656 | tf_op jit(solution)/shard_map/ppermute | solution.py:370
  43.3 10.0 %collective-permute-start.6 = (bf16[12,128,128]{2,1,0:T(8,128)(2,1)S(1)}, bf16[12,128,128]{2,1,0:T(8,128)(2,1)S(1)}, u32[]{:S(2)}, u32[]{:S(2)}) collective-permute-start(bf16[12,128,128]{2,1,0:T(8,128)(2,1)S(1)} %whiten_hour.5.refs_0_), channel_id=1, source_target_pairs={{0,1},{4,5},{8,9},{12,13},{2,3},{6,7},{10,11},{14,15},{1,4},{5,8},... | collective-permute-start | bytes 1179656 | tf_op jit(solution)/shard_map/ppermute | solution.py:370
  43.4 9.9 %collective-permute-start.8 = (bf16[12,128,128]{2,1,0:T(8,128)(2,1)S(1)}, bf16[12,128,128]{2,1,0:T(8,128)(2,1)S(1)}, u32[]{:S(2)}, u32[]{:S(2)}) collective-permute-start(bf16[12,128,128]{2,1,0:T(8,128)(2,1)S(1)} %collective-permute-done.7.refs_2_), channel_id=1, source_target_pairs={{0,1},{4,5},{8,9},{12,13},{1,0},{5,4},{9,8},{13,12},{2,3},{6,7},{1... | collective-permute-start | bytes 1179656 | tf_op jit(solution)/shard_map/ppermute | solution.py:370
  47.5 11.3 %collective-permute-start.15 = (bf16[288,128]{1,0:T(8,128)(2,1)S(1)}, bf16[288,128]{1,0:T(8,128)(2,1)S(1)}, u32[]{:S(2)}, u32[]{:S(2)}) collective-permute-start(bf16[288,128]{1,0:T(8,128)(2,1)S(1)} %get-tuple-element.24), channel_id=1, source_target_pairs={{0,1},{1,2},{2,3},{3,4},{4,5},{5,6},{6,7},{7,8},{8,9},{9,10},{10,1... | collective-permute-start | bytes 221192 | tf_op jit(solution)/shard_map/ppermute | solution.py:375
  49.1 10.3 %collective-permute-start.16 = (bf16[288,128]{1,0:T(8,128)(2,1)S(1)}, bf16[288,128]{1,0:T(8,128)(2,1)S(1)}, u32[]{:S(2)}, u32[]{:S(2)}) collective-permute-start(bf16[288,128]{1,0:T(8,128)(2,1)S(1)} %get-tuple-element.25), channel_id=1, source_target_pairs={{0,2},{1,3},{2,4},{3,5},{4,6},{5,7},{6,8},{7,9},{8,10},{9,11},{10,... | collective-permute-start | bytes 221192 | tf_op jit(solution)/shard_map/ppermute | solution.py:375
  49.1 10.3 %collective-permute-start.17 = (bf16[288,128]{1,0:T(8,128)(2,1)S(1)}, bf16[288,128]{1,0:T(8,128)(2,1)S(1)}, u32[]{:S(2)}, u32[]{:S(2)}) collective-permute-start(bf16[288,128]{1,0:T(8,128)(2,1)S(1)} %get-tuple-element.26), channel_id=1, source_target_pairs={{0,3},{1,4},{2,5},{3,6},{4,7},{5,8},{6,9},{7,10},{8,11},{9,12},{10... | collective-permute-start | bytes 221192 | tf_op jit(solution)/shard_map/ppermute | solution.py:375
  55.8 4.6 %collective-permute-start.12 = (bf16[288,128]{1,0:T(8,128)(2,1)S(1)}, bf16[288,128]{1,0:T(8,128)(2,1)S(1)}, u32[]{:S(2)}, u32[]{:S(2)}) collective-permute-start(bf16[288,128]{1,0:T(8,128)(2,1)S(1)} %get-tuple-element.20), channel_id=1, source_target_pairs={{0,15},{1,0},{2,1},{3,2},{4,3},{5,4},{6,5},{7,6},{8,7},{9,8},{10,9... | collective-permute-start | bytes 221192 | tf_op jit(solution)/shard_map/ppermute | solution.py:375
  57.6 4.5 %collective-permute-start.13 = (bf16[288,128]{1,0:T(8,128)(2,1)S(1)}, bf16[288,128]{1,0:T(8,128)(2,1)S(1)}, u32[]{:S(2)}, u32[]{:S(2)}) collective-permute-start(bf16[288,128]{1,0:T(8,128)(2,1)S(1)} %get-tuple-element.21), channel_id=1, source_target_pairs={{0,14},{1,15},{2,0},{3,1},{4,2},{5,3},{6,4},{7,5},{8,6},{9,7},{10,... | collective-permute-start | bytes 221192 | tf_op jit(solution)/shard_map/ppermute | solution.py:375
  58.8 4.0 %collective-permute-start.14 = (bf16[288,128]{1,0:T(8,128)(2,1)S(1)}, bf16[288,128]{1,0:T(8,128)(2,1)S(1)}, u32[]{:S(2)}, u32[]{:S(2)}) collective-permute-start(bf16[288,128]{1,0:T(8,128)(2,1)S(1)} %get-tuple-element.22), channel_id=1, source_target_pairs={{0,13},{1,14},{2,15},{3,0},{4,1},{5,2},{6,3},{7,4},{8,5},{9,6},{10... | collective-permute-start | bytes 221192 | tf_op jit(solution)/shard_map/ppermute | solution.py:375
